TPU v7x, 32 devices: a whole 2x2x4 slice. The times are simulated.
32 devices in a mesh: pipe: 4 (over x, core), sp: 2 (over y), dp: 4 (over z).
Axes of the slice: x: 2, y: 2, z: 4, core: 2. Of those that a mesh axis runs over, the one named last changes fastest.
Arguments:
- fresh_input: bfloat16 [4, 4, 120, 240, 128], P('pipe', 'dp', 'sp'), may hold values from -6 to 6
- saved_input: bfloat16 [4, 4, 120, 240, 128], P('pipe', 'dp', 'sp'), may hold values from -6 to 6
- output_grad: bfloat16 [4, 4, 120, 240, 128], P('pipe', 'dp', 'sp'), may hold values from -6 to 6
- expand_weight: bfloat16 [4, 128, 768], P('pipe'), may hold values from -0.5 to 0.5
- reduce_weight: bfloat16 [4, 768, 128], P('pipe'), may hold values from -0.21875 to 0.21875
- filter_weight: float32 [4, 2, 120, 128], P('pipe'), may hold values from -6 to 6
- cycle_table: int32 [120], replicated, may hold values from 0 to 119, each once
Outputs:
- next_input: bfloat16 [4, 4, 120, 240, 128], P('pipe', 'dp', 'sp')
- input_grad: bfloat16 [4, 4, 120, 240, 128], P('pipe', 'dp', 'sp')
- expand_grad: float32 [4, 128, 768], P('pipe', None, 'dp')
- reduce_grad: float32 [4, 768, 128], P('pipe', 'dp')
- filter_grad: float32 [4, 2, 120, 128], P('pipe')
Inputs may be any that keep to these rules, and one draw needn't show every extreme that they name: `cycle_table`: each of 0 .. 119 appears once; values 120 or more mark empty cycle slots.
All inputs are finite; a program needn't handle non-finite values.
Results may differ from a plain program's by a relative error of at most 0.025.
Values may be sent and summed in bfloat16 or wider, within the bound.
A program may use at most 192 MiB of HBM per device.

v0:
```python
import math

import jax
import jax.numpy as jnp
from jax import lax
from jax.sharding import PartitionSpec as P

NLAT = 120
NLON = 240


ROOT_HALF = 0.7071067811865476
INV_ROOT_TAU = 0.3989422804014327


def from_behind(block, axis, distance):
    devices = range(lax.axis_size(axis))
    route = [(i - distance, i) for i in devices if i - distance in devices]
    return lax.ppermute(block, axis, route)


def gelu_value(pre_act):
    return 0.5 * pre_act * (1.0 + lax.erf(pre_act * ROOT_HALF))


def gelu_slope(pre_act):
    return (
        0.5 * (1.0 + lax.erf(pre_act * ROOT_HALF))
        + pre_act * jnp.exp(-0.5 * pre_act * pre_act) * INV_ROOT_TAU
    )


def legendre(lat_index, order_index, cycles):
    lat_ok = (lat_index < cycles).astype(jnp.float32)
    order_ok = (order_index < cycles).astype(jnp.float32)
    colatitude = math.pi * (jnp.minimum(lat_index, cycles - 1).astype(jnp.float32) + 0.5) / cycles
    cosine = jnp.cos(colatitude)[None, :]
    sine_value = jnp.sin(colatitude)[None, :]
    order_value = jnp.minimum(order_index, cycles - 1).astype(jnp.float32)[:, None]
    log_start = 0.5 * (
        jnp.log((2.0 * order_value + 1.0) / (4.0 * math.pi))
        + lax.lgamma(2.0 * order_value + 1.0)
        - 2.0 * lax.lgamma(order_value + 1.0)
        - order_value * math.log(4.0)
    ) + order_value * jnp.log(sine_value)
    starting = jnp.exp(log_start)
    zero_rows = jnp.zeros_like(starting)

    def advance(state_pair, degree):
        previous, earlier = state_pair
        degree_value = degree.astype(jnp.float32)
        upper_term = jnp.maximum(4.0 * degree_value * degree_value - 1.0, 0.0)
        ratio_main = jnp.sqrt(
            upper_term / jnp.maximum(degree_value * degree_value - order_value * order_value, 1.0)
        )
        ratio_back = jnp.sqrt(
            jnp.maximum((degree_value - 1.0) ** 2 - order_value * order_value, 0.0)
            / jnp.maximum(4.0 * (degree_value - 1.0) ** 2 - 1.0, 1.0)
        )
        rising = ratio_main * (cosine * previous - ratio_back * earlier)
        current = jnp.where(
            degree_value == order_value,
            starting,
            jnp.where(degree_value > order_value, rising, 0.0),
        )
        return ((current, previous), current)

    _, stacked = lax.scan(advance, (zero_rows, zero_rows), jnp.arange(cycles, dtype=jnp.int32))
    valid_mask = order_ok[:, None] * lat_ok[None, :]
    return jnp.transpose(stacked, (1, 0, 2)) * valid_mask[:, None, :]


def cycle_weights(lat_index, cycles):
    valid_cycle = (lat_index < cycles).astype(jnp.float32)
    colatitude = math.pi * (jnp.minimum(lat_index, cycles - 1).astype(jnp.float32) + 0.5) / cycles
    return math.pi / cycles * jnp.sin(colatitude) * valid_cycle


def fourier_tables(order_index, cycles, points):
    valid_order = (order_index < cycles).astype(jnp.float32)[None, :]
    order_value = jnp.minimum(order_index, cycles - 1)
    longitude = jnp.arange(points, dtype=jnp.int32)
    phase_angle = (
        2.0
        * math.pi
        / points
        * (longitude[:, None] * order_value[None, :] % points).astype(jnp.float32)
    )
    scaled = valid_order * (2.0 * math.pi / points)
    forward = jnp.concatenate(
        [jnp.cos(phase_angle) * scaled, -jnp.sin(phase_angle) * scaled], axis=1
    )
    order_scale = jnp.where(order_value == 0, 1.0, 2.0)[None, :] * valid_order / (2.0 * math.pi)
    inverse = jnp.concatenate(
        [jnp.cos(phase_angle) * order_scale, -jnp.sin(phase_angle) * order_scale], axis=1
    ).T
    return (forward.astype(jnp.bfloat16), inverse.astype(jnp.bfloat16))


def joint_orders(coeffs):
    return lax.all_to_all(coeffs, "sp", split_axis=3, concat_axis=1, tiled=True)


def joint_cycles(values):
    return lax.all_to_all(values, "sp", split_axis=1, concat_axis=3, tiled=True)


def spectral_pass(tokens, filt, forward, analysis, synthesis, inverse, to_orders, to_cycles):
    batch_count, row_count, points, chan_count = tokens.shape
    order_count = forward.shape[1] // 2
    coeffs = jnp.einsum(
        "sjnc,nk->sjkc", tokens, forward, preferred_element_type=jnp.float32
    ).astype(jnp.bfloat16)
    coeffs = coeffs.reshape(batch_count, row_count, 2, order_count, chan_count)
    arrived = to_orders(coeffs)
    spectra = jnp.einsum("tlj,sjrtc->strlc", analysis, arrived, preferred_element_type=jnp.float32)
    real_part = filt[0] * spectra[:, :, 0] - filt[1] * spectra[:, :, 1]
    imag_part = filt[0] * spectra[:, :, 1] + filt[1] * spectra[:, :, 0]
    filtered = jnp.stack([real_part, imag_part], axis=2).astype(jnp.bfloat16)
    values = jnp.einsum(
        "tlj,strlc->sjrtc", synthesis, filtered, preferred_element_type=jnp.float32
    ).astype(jnp.bfloat16)
    returned = to_cycles(values).reshape(batch_count, row_count, 2 * order_count, chan_count)
    spatial = jnp.einsum("sjkc,kn->sjnc", returned, inverse, preferred_element_type=jnp.float32)
    return (spatial, spectra)


def mlp_pass(tokens, spatial, expand, contract, cycle_mask):
    grid_shape = tokens.shape
    flat_rows = (tokens.astype(jnp.float32) + spatial).reshape(-1, grid_shape[-1])
    mixed_b = flat_rows.astype(jnp.bfloat16)
    hidden_pre = jnp.dot(mixed_b, expand, preferred_element_type=jnp.float32)
    hidden = gelu_value(hidden_pre).astype(jnp.bfloat16)
    result = flat_rows + jnp.dot(hidden, contract, preferred_element_type=jnp.float32)
    result = (result.reshape(grid_shape) * cycle_mask[:, None, None]).astype(jnp.bfloat16)
    return (result, mixed_b, hidden_pre, hidden)


def backward_rows(cotangent, cycle_mask, mixed_b, hidden_pre, hidden, expand, contract):
    chan_count = cotangent.shape[-1]
    masked = (cotangent * cycle_mask.astype(jnp.bfloat16)[:, None, None]).reshape(-1, chan_count)
    grad_reduce = jnp.dot(hidden.T, masked, preferred_element_type=jnp.float32)
    grad_hidden = jnp.dot(masked, contract.T, preferred_element_type=jnp.float32)
    grad_pre = (grad_hidden * gelu_slope(hidden_pre)).astype(jnp.bfloat16)
    grad_expand = jnp.dot(mixed_b.T, grad_pre, preferred_element_type=jnp.float32)
    grad_mixed = masked.astype(jnp.float32) + jnp.dot(
        grad_pre, expand.T, preferred_element_type=jnp.float32
    )
    return (grad_mixed, grad_expand, grad_reduce)


def on_device(
    fresh_input, saved_input, output_grad, expand_weight, reduce_weight, filter_weight, cycle_table
):
    slot_count = fresh_input.shape[2]
    position = lax.axis_index("sp")
    order_table = jnp.arange(slot_count * lax.axis_size("sp"), dtype=jnp.int32)
    own_cycles = lax.dynamic_slice_in_dim(cycle_table, position * slot_count, slot_count)
    own_orders = lax.dynamic_slice_in_dim(order_table, position * slot_count, slot_count)
    cycle_mask = (own_cycles < NLAT).astype(jnp.float32)
    table = legendre(cycle_table, own_orders, NLAT)
    analysis = (table * cycle_weights(cycle_table, NLAT)[None, None, :]).astype(jnp.bfloat16)
    synthesis = table.astype(jnp.bfloat16)
    forward, inverse = fourier_tables(order_table, NLAT, NLON)
    filt = filter_weight[0]
    expand = expand_weight[0]
    contract = reduce_weight[0]
    fresh = fresh_input[0, 0]
    saved = saved_input[0, 0]
    spatial, spectra = spectral_pass(
        jnp.stack([fresh, saved]),
        filt,
        forward,
        analysis,
        synthesis,
        inverse,
        joint_orders,
        joint_cycles,
    )
    fresh_spatial = spatial[0]
    saved_spatial = spatial[1]
    saved_spectra = spectra[1]
    block = mlp_pass(fresh, fresh_spatial, expand, contract, cycle_mask)[0]
    next_input = from_behind(block[None, None], "pipe", 1)
    _, mixed_b, hidden_pre, hidden = mlp_pass(saved, saved_spatial, expand, contract, cycle_mask)
    grad_mixed, grad_expand, grad_reduce = backward_rows(
        output_grad[0, 0], cycle_mask, mixed_b, hidden_pre, hidden, expand, contract
    )
    grid_shape = saved.shape
    row_count, points, chan_count = grid_shape
    order_count = forward.shape[1] // 2
    grad_rows = grad_mixed.reshape(grid_shape).astype(jnp.bfloat16)
    grad_values = jnp.einsum(
        "jnc,kn->jkc", grad_rows, inverse, preferred_element_type=jnp.float32
    ).astype(jnp.bfloat16)
    grad_values = grad_values.reshape(row_count, 2, order_count, chan_count)
    arrived = lax.all_to_all(grad_values, "sp", split_axis=2, concat_axis=0, tiled=True)
    grad_filtered = jnp.einsum(
        "tlj,jrtc->trlc", synthesis, arrived, preferred_element_type=jnp.float32
    )
    filter_real = jnp.sum(
        grad_filtered[:, 0] * saved_spectra[:, 0] + grad_filtered[:, 1] * saved_spectra[:, 1],
        axis=0,
    )
    filter_imag = jnp.sum(
        grad_filtered[:, 1] * saved_spectra[:, 0] - grad_filtered[:, 0] * saved_spectra[:, 1],
        axis=0,
    )
    grad_spectra = jnp.stack(
        [
            filt[0] * grad_filtered[:, 0] + filt[1] * grad_filtered[:, 1],
            filt[0] * grad_filtered[:, 1] - filt[1] * grad_filtered[:, 0],
        ],
        axis=1,
    ).astype(jnp.bfloat16)
    grad_coeffs = jnp.einsum(
        "tlj,trlc->jrtc", analysis, grad_spectra, preferred_element_type=jnp.float32
    ).astype(jnp.bfloat16)
    returned = lax.all_to_all(grad_coeffs, "sp", split_axis=0, concat_axis=2, tiled=True)
    grad_tokens = jnp.einsum(
        "jkc,nk->jnc",
        returned.reshape(row_count, 2 * order_count, chan_count),
        forward,
        preferred_element_type=jnp.float32,
    )
    input_grad = (
        (grad_mixed.reshape(grid_shape) + grad_tokens) * cycle_mask[:, None, None]
    ).astype(jnp.bfloat16)
    sent_back = from_behind(input_grad[None, None], "pipe", -1)
    filter_grad = lax.psum(jnp.stack([filter_real, filter_imag]), ("sp", "dp"))
    summed = (
        lax.psum(grad_expand.astype(jnp.bfloat16), "sp").astype(jnp.float32),
        lax.psum(grad_reduce.astype(jnp.bfloat16), "sp").astype(jnp.float32),
    )
    expand_grad, reduce_grad = (
        lax.psum_scatter(
            summed[0].astype(jnp.bfloat16), "dp", scatter_dimension=1, tiled=True
        ).astype(jnp.float32),
        lax.psum_scatter(
            summed[1].astype(jnp.bfloat16), "dp", scatter_dimension=0, tiled=True
        ).astype(jnp.float32),
    )
    return (next_input, sent_back, expand_grad[None], reduce_grad[None], filter_grad[None])


def solution(mesh):
    return jax.shard_map(
        on_device,
        mesh=mesh,
        in_specs=(
            P("pipe", "dp", "sp", None, None),
            P("pipe", "dp", "sp", None, None),
            P("pipe", "dp", "sp", None, None),
            P("pipe", None, None),
            P("pipe", None, None),
            P("pipe", None, None, None),
            P(),
        ),
        out_specs=(
            P("pipe", "dp", "sp", None, None),
            P("pipe", "dp", "sp", None, None),
            P("pipe", None, "dp"),
            P("pipe", "dp", None),
            P("pipe", None, None, None),
        ),
        check_vma=False,
    )
```

profile of v0, /device:TPU:1, one launch (start us, length us, event | category | flops | bytes accessed | tf_op | source)
XLA Modules:
  0.0 804.7 jit_solution(4464652124420981998)
XLA Ops:
  8.7 5.3 fusion.33
  14.0 8.9 %copy.39 = bf16[2,60,2,120,128]{4,2,1,0,3:T(2,128)(2,1)} copy(bf16[2,60,2,120,128]{4,3,2,1,0:T(8,128)(2,1)S(1)} %bitcast.168) | data formatting | bytes 14745600 | tf_op jit(solution)/shard_map/reshape | solution.py:114
  22.9 6.9 all-to-all-start
  30.1 240.9 %while.18 = (s32[]{:T(128)}, f32[60,120]{1,0:T(8,128)S(1)}, f32[60,120]{1,0:T(8,128)S(1)}, f32[120,60,120]{2,1,0:T(8,128)}, s32[120]{0:T(128)S(1)}, /*index=5*/f...) while((s32[]{:T(128)}, f32[60,120]{1,0:T(8,128)S(1)}, ...), condition=%wide.region_1.2_spmd.clone, body=%wide.region_0.1_spmd.clone.sunk | while | flops 65294 | bytes 151427 | solution.py:68
  39.4 0.7 bitcast_dynamic-update-slice_fusion.2
  43.4 0.7 bitcast_dynamic-update-slice_fusion.2
  63.5 0.7 bitcast_dynamic-update-slice_fusion.2
  87.6 0.7 bitcast_dynamic-update-slice_fusion.2
  115.7 0.7 bitcast_dynamic-update-slice_fusion.2
  119.7 0.7 bitcast_dynamic-update-slice_fusion.2
  123.7 0.7 bitcast_dynamic-update-slice_fusion.2
  127.7 0.7 bitcast_dynamic-update-slice_fusion.2
  129.7 0.7 bitcast_dynamic-update-slice_fusion.2
  151.8 0.7 bitcast_dynamic-update-slice_fusion.2
  169.9 0.7 bitcast_dynamic-update-slice_fusion.2
  171.9 0.7 bitcast_dynamic-update-slice_fusion.2
  177.9 0.7 bitcast_dynamic-update-slice_fusion.2
  220.1 0.7 bitcast_dynamic-update-slice_fusion.2
  271.9 4.3 broadcast_multiply_fusion
  276.2 3.9 fusion.61
  280.1 7.4 copy.41
  287.5 12.1 %convolution_bitcast_fusion = f32[2,60,2,120,128]{4,3,2,0,1:T(8,128)} fusion(bf16[2,120,2,60,128]{4,2,3,1,0:T(2,128)(2,1)} %bitcast.162, bf16[60,120,120,1,1]{2,0,1,4,3:T(8,128)(2,1)S(1)} %get-tuple-element.230), kind=kOutput, calls=%fused_computation.24 | convolution fusion | flops 884736000 | bytes 23846400 | tf_op jit(solution)/shard_map/tlj,sjrtc->strlc/dot_general | solution.py:116
  299.6 8.6 %subtract_convert_fusion = (bf16[2,60,1,120,128]{4,3,2,0,1:T(8,128)(2,1)}, bf16[2,60,1,120,128]{4,3,2,0,1:T(8,128)(2,1)}) fusion(f32[2,60,2,120,128]{4,3,2,0,1:T(8,128)} %convolution_bitcast_fusion, f32[120,128]{1,0:T(8,128)S(1)} %get-tuple-element.234, f32[120,128]{1,0:T(8,128)S(1)} %get-tuple-element.233), kind=kLoop, calls=%fused_computation.48 | loop fusion | flops 14745600 | bytes 22241280 | tf_op jit(solution)/shard_map/convert.6
  308.2 11.1 %convert_bitcast_fusion = bf16[2,120,2,60,128]{4,1,2,0,3:T(8,128)(2,1)} fusion(bf16[2,60,1,120,128]{4,3,2,0,1:T(8,128)(2,1)} %get-tuple-element.220, bf16[2,60,1,120,128]{4,3,2,0,1:T(8,128)(2,1)} %get-tuple-element.219, bf16[60,120,120,1,1]{2,0,1,4,3:T(8,128)(2,1)S(1)} %copy-done.7), kind=kOutput, calls=%fused_computation.46 | convolution fusion | flops 892108800 | bytes 16473600 | tf_op jit(solution)/shard_map/tlj,strlc->sjrtc/dot_general | solution.py:120
  319.2 11.9 %copy.45 = bf16[2,120,2,60,128]{4,2,0,3,1:T(2,128)(2,1)} copy(bf16[2,120,2,60,128]{4,1,2,0,3:T(8,128)(2,1)} %convert_bitcast_fusion) | data formatting | bytes 14745600 | tf_op jit(solution)/shard_map/convert_element_type | solution.py:122
  331.1 6.7 all-to-all-start.1
  337.8 9.4 %bitcast_multiply_fusion = bf16[14400,128]{1,0:T(8,128)(2,1)} fusion(bf16[1,1,60,240,128]{4,3,2,1,0:T(8,128)(2,1)} %param.11, bf16[14400]{0:T(1024)(128)(2,1)S(1)} %mul.489), kind=kLoop, calls=%fused_computation.58 | loop fusion | flops 1843200 | bytes 7401600 | tf_op jit(solution)/shard_map/mul | solution.py:141
  347.2 6.6 slice_bitcast_fusion
  353.8 65.8 %all-to-all-done.1 = bf16[2,120,2,60,128]{4,2,0,3,1:T(2,128)(2,1)} async-done(((bf16[2,120,2,60,128]{4,2,0,3,1:T(2,128)(2,1)}), bf16[2,120,2,60,128]{4,2,0,3,1:T(2,128)(2,1)}, u32[]{:S(2)}, u32[]{:S(2)}) %all-to-all-start.1) | async-done | bytes 7372832 | tf_op jit(solution)/shard_map/all_to_all | solution.py:105
  419.6 11.0 %copy.47 = bf16[2,60,2,2,60,128]{5,0,4,3,2,1:T(2,128)(2,1)S(1)} copy(bf16[2,60,2,2,60,128]{5,2,0,4,1,3:T(2,128)(2,1)} %bitcast.25) | data formatting | bytes 14745600 | tf_op jit(solution)/shard_map/all_to_all | solution.py:105
  430.6 7.3 fusion.30
  438.0 12.9 %fusion.100 = (f32[1,60,240,128]{3,2,1,0:T(8,128)S(1)}, bf16[1,60,240,128]{3,2,1,0:T(8,128)(2,1)}, bf16[1,60,240,128]{3,2,1,0:T(8,128)(2,1)S(1)}, f32[1,60,240,128]{3,2,1,0:T(8,128)}) fusion(f32[2,60,240,128]{3,2,1,0:T(8,128)} %fusion.30, bf16[1,1,60,240,128]{4,3,2,1,0:T(8,128)(2,1)} %param.9, bf16[1,1,60,240,128]{4,3,2,1,0:T(8,128)(2,1)} %param.10), kind=kLoop, calls=%fused_computation.174 | loop fusion | flops 11059200 | bytes 44236800 | tf_op jit(solution)/shard_map/slice | solution.py:181
  450.9 3.7 fusion.22
  454.6 17.0 %fusion.65 = f32[14400,768]{1,0:T(8,128)} fusion(bf16[14400,128]{1,0:T(8,128)(2,1)S(1)} %bitcast.163, bf16[1,128,768]{2,1,0:T(8,128)(2,1)S(1)} %copy-done), kind=kOutput, calls=%fused_computation.84 | convolution fusion | flops 2831155200 | bytes 48119808 | tf_op jit(solution)/shard_map/dot_general | solution.py:132
  471.6 31.0 %fusion.7 = bf16[14400,768]{1,0:T(8,128)(2,1)} fusion(f32[14400,768]{1,0:T(8,128)} %fusion.65, bf16[14400,128]{1,0:T(8,128)(2,1)} %bitcast.170, bf16[1,768,128]{2,1,0:T(8,128)(2,1)S(1)} %copy-done.20), kind=kOutput, calls=%fused_computation.14 | convolution fusion | flops 2941747200 | bytes 70238208 | tf_op jit(solution)/shard_map/dot_general | solution.py:143
  502.6 10.9 %convolution_add_fusion = f32[14400,128]{1,0:T(8,128)S(1)} fusion(bf16[14400,768]{1,0:T(8,128)(2,1)} %fusion.7, bf16[14400,128]{1,0:T(8,128)(2,1)S(1)} %copy-done.2, bf16[1,128,768]{2,1,0:T(8,128)(2,1)S(1)} %copy-done), kind=kOutput, calls=%fused_computation.22 | convolution fusion | flops 2834841600 | bytes 33374208 | tf_op jit(solution)/shard_map/dot_general | solution.py:146
  513.6 1.2 fusion.48
  514.7 1.8 copy-done.1
  516.5 4.6 copy.50
  521.2 5.4 all-to-all-start.2
  526.6 16.7 %fusion.11 = f32[14400,128]{1,0:T(8,128)} fusion(bf16[14400,128]{1,0:T(8,128)(2,1)} %bitcast.173, f32[14400,128]{1,0:T(8,128)} %bitcast.167, bf16[14400,128]{1,0:T(8,128)(2,1)} %bitcast.172, bf16[1,768,128]{2,1,0:T(8,128)(2,1)S(1)} %copy-done.20, bf16[1,128,768]{2,1,0:T(8,128)(2,1)S(1)} %copy-done), kind=kOutput, calls=%fused_computation.21 | convolution fusion | flops 5723136000 | bytes 22511616 | tf_op jit(solution)/shard_map/dot_general | solution.py:134
  543.3 5.6 multiply_convert_fusion.6
  548.9 4.5 collective-permute-start
  553.4 14.0 %all-to-all-done.2 = bf16[60,2,120,128]{3,1,0,2:T(2,128)(2,1)} async-done(((bf16[60,2,120,128]{3,1,0,2:T(2,128)(2,1)}), bf16[60,2,120,128]{3,1,0,2:T(2,128)(2,1)}, u32[]{:S(2)}, u32[]{:S(2)}) %all-to-all-start.2) | async-done | bytes 3686432 | tf_op jit(solution)/shard_map/all_to_all | solution.py:197
  567.4 4.7 copy.52
  572.2 1.9 fusion.45
  574.4 2.3 add_reduce_fusion
  576.6 4.8 convert_bitcast_fusion.1
  581.4 4.8 copy.56
  586.2 5.4 all-to-all-start.3
  591.7 14.8 %convolution_convert_fusion = bf16[128,768]{0,1:T(8,128)(2,1)} fusion(bf16[14400,128]{1,0:T(8,128)(2,1)} %fusion.22, bf16[14400,768]{1,0:T(8,128)(2,1)} %fusion.7), kind=kOutput, calls=%fused_computation.76 | convolution fusion | flops 2831253504 | bytes 26001408 | tf_op jit(solution)/shard_map/dot_general | solution.py:145
  606.6 25.1 %all-to-all-done.3 = bf16[120,2,60,128]{3,1,2,0:T(2,128)(2,1)} async-done(((bf16[120,2,60,128]{3,1,2,0:T(2,128)(2,1)}), bf16[120,2,60,128]{3,1,2,0:T(2,128)(2,1)}, u32[]{:S(2)}, u32[]{:S(2)}) %all-to-all-start.3) | async-done | bytes 3686432 | tf_op jit(solution)/shard_map/all_to_all | solution.py:219
  631.6 5.1 copy.57
  636.7 6.6 reshape.336
  643.3 7.4 fusion.36
  650.7 4.8 collective-permute-start.1
  655.5 20.0 %fusion.57 = bf16[768,128]{1,0:T(8,128)(2,1)} fusion(bf16[14400,128]{1,0:T(8,128)(2,1)S(1)} %copy-done.3, f32[14400,768]{1,0:T(8,128)} %fusion.65), kind=kOutput, calls=%fused_computation.75 | convolution fusion | flops 2886549504 | bytes 48119808 | tf_op jit(solution)/shard_map/dot_general | solution.py:142
  675.6 18.7 %reduce-scatter.5.cloned.1.call-done = bf16[192,128]{1,0:T(8,128)(2,1)} async-done(((bf16[768,128]{1,0:T(8,128)(2,1)}), bf16[192,128]{1,0:T(8,128)(2,1)}) %reduce-scatter.5.cloned.1.call-update) | async-done | bytes 49168 | tf_op jit(solution)/shard_map/reduce_scatter | solution.py:239
  694.4 23.6 %all-reduce.6.cloned.1.call-done = (bf16[128,192]{0,1:T(8,128)(2,1)}, bf16[192,128]{1,0:T(8,128)(2,1)}) async-done(((bf16[128,192]{0,1:T(8,128)(2,1)}, bf16[192,128]{1,0:T(8,128)(2,1)}), (bf16[128,192]{0,1:T(8,128)(2,1)}, bf16[192,128]{1,0:T(8,128)(2,1)})) %all-reduce.6.cloned.1.call-update) | async-done | bytes 98320 | tf_op jit(solution)/shard_map/psum | solution.py:232
  718.0 1.4 bitcast_convert_fusion.1
  720.1 1.4 bitcast_convert_fusion
  721.6 66.9 %all-reduce.4.cloned.1.call-done = f32[1,2,120,128]{3,2,1,0:T(8,128)} async-done(((f32[1,2,120,128]{3,2,1,0:T(8,128)}), f32[1,2,120,128]{3,2,1,0:T(8,128)}) %all-reduce.4.cloned.1.call-update) | async-done | bytes 122896 | tf_op jit(solution)/shard_map/psum | solution.py:230
  788.4 4.1 copy.115
  792.5 4.2 copy.116
  (543 shorter events, 153.2 us)
Async XLA Ops:
  8.0 446.6 %copy-start = (bf16[1,128,768]{2,1,0:T(8,128)(2,1)S(1)}, bf16[1,128,768]{2,1,0:T(8,128)(2,1)}, u32[]{:S(2)}) copy-start(bf16[1,128,768]{2,1,0:T(8,128)(2,1)} %param.12) | copy-start | bytes 589828
  8.6 5.3 copy-start.12
  8.7 5.3 copy-start.14
  22.9 7.1 copy-start.19
  22.9 249.0 %copy-start.16 = (f32[1,2,120,128]{3,2,1,0:T(8,128)S(1)}, f32[1,2,120,128]{3,2,1,0:T(8,128)}, u32[]{:S(2)}) copy-start(f32[1,2,120,128]{3,2,1,0:T(8,128)} %param.14) | copy-start | bytes 368644
  22.9 257.3 %all-to-all-start = ((bf16[2,60,2,120,128]{4,2,1,0,3:T(2,128)(2,1)}), bf16[2,60,2,120,128]{4,2,1,0,3:T(2,128)(2,1)}, u32[]{:S(2)}, u32[]{:S(2)}) async-start(bf16[2,60,2,120,128]{4,2,1,0,3:T(2,128)(2,1)} %copy.39), calls=%async_computation | async-start | bytes 14745600 | tf_op jit(solution)/shard_map/all_to_all | solution.py:101
  271.7 4.5 copy-start.5
  271.9 27.8 %copy-start.8 = (f32[120,128]{1,0:T(8,128)}, f32[120,128]{1,0:T(8,128)S(1)}, u32[]{:S(2)}) copy-start(f32[120,128]{1,0:T(8,128)S(1)} %get-tuple-element.233) | copy-start | bytes 184324
  271.9 27.8 %copy-start.10 = (f32[120,128]{1,0:T(8,128)}, f32[120,128]{1,0:T(8,128)S(1)}, u32[]{:S(2)}) copy-start(f32[120,128]{1,0:T(8,128)S(1)} %get-tuple-element.234) | copy-start | bytes 184324
  299.6 8.6 %copy-start.7 = (bf16[60,120,120,1,1]{2,0,1,4,3:T(8,128)(2,1)S(1)}, bf16[60,120,120,1,1]{2,0,1,4,3:T(8,128)(2,1)}, u32[]{:S(2)}) copy-start(bf16[60,120,120,1,1]{2,0,1,4,3:T(8,128)(2,1)} %get-tuple-element.231) | copy-start | bytes 5184004
  331.1 88.5 %all-to-all-start.1 = ((bf16[2,120,2,60,128]{4,2,0,3,1:T(2,128)(2,1)}), bf16[2,120,2,60,128]{4,2,0,3,1:T(2,128)(2,1)}, u32[]{:S(2)}, u32[]{:S(2)}) async-start(bf16[2,120,2,60,128]{4,2,0,3,1:T(2,128)(2,1)} %copy.45), calls=%async_computation.1 | async-start | bytes 14745600 | tf_op jit(solution)/shard_map/all_to_all | solution.py:105
  454.6 17.1 %copy-start.20 = (bf16[1,768,128]{2,1,0:T(8,128)(2,1)S(1)}, bf16[1,768,128]{2,1,0:T(8,128)(2,1)}, u32[]{:S(2)}) copy-start(bf16[1,768,128]{2,1,0:T(8,128)(2,1)} %param.13) | copy-start | bytes 589828
  471.6 31.0 %copy-start.2 = (bf16[14400,128]{1,0:T(8,128)(2,1)S(1)}, bf16[14400,128]{1,0:T(8,128)(2,1)}, u32[]{:S(2)}) copy-start(bf16[14400,128]{1,0:T(8,128)(2,1)} %bitcast_multiply_fusion) | copy-start | bytes 11059204
  513.6 3.0 copy-start.1
  521.2 46.2 %all-to-all-start.2 = ((bf16[60,2,120,128]{3,1,0,2:T(2,128)(2,1)}), bf16[60,2,120,128]{3,1,0,2:T(2,128)(2,1)}, u32[]{:S(2)}, u32[]{:S(2)}) async-start(bf16[60,2,120,128]{3,1,0,2:T(2,128)(2,1)} %copy.50), calls=%async_computation.2 | async-start | bytes 7372800 | tf_op jit(solution)/shard_map/all_to_all | solution.py:197
  526.6 16.7 %copy-start.18 = (f32[60]{0:T(128)S(1)}, f32[60]{0:T(128)}, u32[]{:S(2)}) copy-start(f32[60]{0:T(128)} %get-tuple-element.212) | copy-start | bytes 724
  548.9 23.3 %copy-start.4 = (bf16[60,120,120,1]{2,0,1,3:T(8,128)(2,1)S(1)}, bf16[60,120,120,1]{2,0,1,3:T(8,128)(2,1)}, u32[]{:S(2)}) copy-start(bf16[60,120,120,1]{2,0,1,3:T(8,128)(2,1)} %get-tuple-element.232) | copy-start | bytes 5184004
  548.9 172.7 %collective-permute-start = (bf16[1,1,60,240,128]{4,3,2,1,0:T(8,128)(2,1)}, bf16[1,1,60,240,128]{4,3,2,1,0:T(8,128)(2,1)}, u32[]{:S(2)}, u32[]{:S(2)}) collective-permute-start(bf16[1,1,60,240,128]{4,3,2,1,0:T(8,128)(2,1)} %multiply_convert_fusion.6), channel_id=1, source_target_pairs={{0,8},{8,16},{16,24},{1,9},{9,17},{17,25},{2,10},{10,18},{18,26},{... | collective-permute-start | bytes 11059208 | tf_op jit(solution)/shard_map/ppermute | solution.py:19
  567.4 6.7 slice-start
  572.2 2.2 slice-start.1
  572.2 2.2 copy-start.9
  572.2 2.2 copy-start.11
  574.4 2.3 copy-start.6
  586.2 45.4 %all-to-all-start.3 = ((bf16[120,2,60,128]{3,1,2,0:T(2,128)(2,1)}), bf16[120,2,60,128]{3,1,2,0:T(2,128)(2,1)}, u32[]{:S(2)}, u32[]{:S(2)}) async-start(bf16[120,2,60,128]{3,1,2,0:T(2,128)(2,1)} %copy.56), calls=%async_computation.3 | async-start | bytes 7372800 | tf_op jit(solution)/shard_map/all_to_all | solution.py:219
  591.7 83.9 %reduce-scatter.3.cloned.1.call-start = ((), (), s32[]{:S(2)}) async-start(), calls=%async_computation.7 | async-start | bytes 245760 | tf_op jit(solution)/shard_map/reduce_scatter | solution.py:236
  606.5 87.8 %reduce-scatter.5.cloned.1.call-start = ((), (), s32[]{:S(2)}) async-start(), calls=%async_computation.8 | async-start | bytes 245760 | tf_op jit(solution)/shard_map/reduce_scatter | solution.py:239
  636.7 6.6 copy-start.13
  636.7 6.6 copy-start.15
  643.3 12.2 %copy-start.3 = (bf16[14400,128]{1,0:T(8,128)(2,1)S(1)}, bf16[14400,128]{1,0:T(8,128)(2,1)}, u32[]{:S(2)}) copy-start(bf16[14400,128]{1,0:T(8,128)(2,1)} %bitcast_multiply_fusion) | copy-start | bytes 11059204
  650.7 70.9 %collective-permute-start.1 = (bf16[1,1,60,240,128]{4,3,2,1,0:T(8,128)(2,1)}, bf16[1,1,60,240,128]{4,3,2,1,0:T(8,128)(2,1)}, u32[]{:S(2)}, u32[]{:S(2)}) collective-permute-start(bf16[1,1,60,240,128]{4,3,2,1,0:T(8,128)(2,1)} %fusion.36), channel_id=1, source_target_pairs={{8,0},{16,8},{24,16},{9,1},{17,9},{25,17},{10,2},{18,10},{26,18},{... | collective-permute-start | bytes 11059208 | tf_op jit(solution)/shard_map/ppermute | solution.py:19
  675.5 42.5 %all-reduce.6.cloned.1.call-start = ((), (), s32[]{:S(2)}) async-start(), calls=%async_computation.9 | async-start | bytes 196608 | tf_op jit(solution)/shard_map/psum | solution.py:232
  694.3 94.1 %all-reduce.4.cloned.1.call-start = ((), (), s32[]{:S(2)}) async-start(), calls=%async_computation.6 | async-start | bytes 245760 | tf_op jit(solution)/shard_map/psum | solution.py:230
  792.5 4.2 copy-start.17
Sparse Core Ops, SparseCore 0:
  606.6 20.2 reduce-scatter.2
  675.6 18.6 reduce-scatter.4
  696.6 21.3 all-reduce.5
Sparse Core Ops, SparseCore 1:
  720.2 68.2 all-reduce.3
where the time goes:
time: 813 us; the launch traced here: 805 us
  waiting for transfers between devices  214 us (26%)
  matrix products  161 us (20%)
  local copies, waits for them, and re-layouts  153 us (19%)
  other arithmetic  146 us (18%)
  loops' own time  80.9 us (10%)
  starting transfers between devices  34 us (4%)
  between operations  15.8 us (2%)
    dynamic_update_slice x120, other arithmetic, legendre(): lax.scan(advance, (zero_rows, zero_rows), jnp.arange(cycles, dtype=jnp.in...  87.6 us
    another operation x1, loops' own time, legendre(): lax.scan(advance, (zero_rows, zero_rows), jnp.arange(cycles, dtype=jnp.in...  80.9 us
    dynamic_slice x120, local copies, waits for them, and re-layouts, legendre(): lax.scan(advance, (zero_rows, zero_rows), jnp.arange(cycles, dtype=jnp.in...  69.9 us
    psum x1, waiting for transfers between devices, on_device(): filter_grad = lax.psum(jnp.stack([filter_real, filter_imag]), ('sp', 'dp'))  66.9 us
    all_to_all x1, waiting for transfers between devices, joint_cycles(): return lax.all_to_all(values, 'sp', split_axis=1, concat_axis=3, tiled=True)  65.8 us
    dot_general x1, matrix products, backward_rows(): jnp.dot(masked, contract.T, preferred_element_type=jnp.float32)  31 us
    all_to_all x1, waiting for transfers between devices, on_device(): lax.all_to_all(grad_coeffs, 'sp', split_axis=0, concat_axis=2, tiled=True)  25.1 us
    psum x1, waiting for transfers between devices, on_device(): lax.psum(grad_expand.astype(jnp.bfloat16), 'sp').astype(jnp.float32)  23.6 us
  transfers between devices with their start and end apart: 10, of which 6 were waited for; matrix products, arithmetic and copies ran while one was open for 35% of the time, Pallas kernels for 0%

commit v1 on v0

--- a/solution.py
+++ b/solution.py
@@ -1,8 +1,11 @@
+import functools
 import math
 
 import jax
 import jax.numpy as jnp
 from jax import lax
+from jax.experimental import pallas as pl
+from jax.experimental.pallas import tpu as pltpu
 from jax.sharding import PartitionSpec as P
 
 NLAT = 120
@@ -243,9 +246,329 @@
     return (next_input, sent_back, expand_grad[None], reduce_grad[None], filter_grad[None])
 
 
+VMEM_BYTES = 58 * 1024 * 1024
+
+
+def interleave(table, order_count):
+    rows = table.shape[0]
+    return table.reshape(rows, 2, order_count).transpose(0, 2, 1).reshape(rows, 2 * order_count)
+
+
+def recursion_kernel(cycles, main_ref, back_ref, start_ref, cos_ref, weight_ref, valid_ref,
+                     analysis_ref, synthesis_ref, table_ref):
+    order_count = start_ref.shape[0]
+    slots = start_ref.shape[1]
+    orders = valid_ref[...]
+    start = start_ref[...]
+    cosine = jnp.broadcast_to(cos_ref[...], (order_count, slots))
+    previous = jnp.zeros_like(start)
+    earlier = jnp.zeros_like(start)
+    for degree in range(cycles):
+        rising = main_ref[:, degree : degree + 1] * (
+            cosine * previous - back_ref[:, degree : degree + 1] * earlier
+        )
+        current = jnp.where(
+            orders == float(degree), start, jnp.where(orders < float(degree), rising, 0.0)
+        )
+        table_ref[:, degree, :] = current
+        previous, earlier = current, previous
+    weight = weight_ref[...]
+
+    @pl.loop(0, order_count)
+    def _(at):
+        rows = table_ref[at]
+        analysis_ref[at] = (rows * weight).astype(jnp.bfloat16)
+        synthesis_ref[at] = rows.astype(jnp.bfloat16)
+
+
+def legendre_tables(lat_index, order_index, cycles):
+    lat_ok = (lat_index < cycles).astype(jnp.float32)
+    order_ok = (order_index < cycles).astype(jnp.float32)
+    colatitude = math.pi * (jnp.minimum(lat_index, cycles - 1).astype(jnp.float32) + 0.5) / cycles
+    cosine = jnp.cos(colatitude)[None, :]
+    sine_value = jnp.sin(colatitude)[None, :]
+    order_value = jnp.minimum(order_index, cycles - 1).astype(jnp.float32)[:, None]
+    log_start = 0.5 * (
+        jnp.log((2.0 * order_value + 1.0) / (4.0 * math.pi))
+        + lax.lgamma(2.0 * order_value + 1.0)
+        - 2.0 * lax.lgamma(order_value + 1.0)
+        - order_value * math.log(4.0)
+    ) + order_value * jnp.log(sine_value)
+    starting = jnp.exp(log_start) * (order_ok[:, None] * lat_ok[None, :])
+    degree = jnp.arange(cycles, dtype=jnp.float32)[None, :]
+    upper_term = jnp.maximum(4.0 * degree * degree - 1.0, 0.0)
+    ratio_main = jnp.sqrt(
+        upper_term / jnp.maximum(degree * degree - order_value * order_value, 1.0)
+    )
+    ratio_back = jnp.sqrt(
+        jnp.maximum((degree - 1.0) ** 2 - order_value * order_value, 0.0)
+        / jnp.maximum(4.0 * (degree - 1.0) ** 2 - 1.0, 1.0)
+    )
+    weight = cycle_weights(lat_index, cycles)[None, :]
+    order_count, slots = starting.shape
+    shape = (order_count, cycles, slots)
+    return pl.pallas_call(
+        functools.partial(recursion_kernel, cycles),
+        out_shape=[jax.ShapeDtypeStruct(shape, jnp.bfloat16)] * 2,
+        in_specs=[pl.BlockSpec(memory_space=pltpu.VMEM)] * 6,
+        out_specs=[pl.BlockSpec(memory_space=pltpu.VMEM)] * 2,
+        scratch_shapes=[pltpu.VMEM(shape, jnp.float32)],
+        compiler_params=pltpu.CompilerParams(vmem_limit_bytes=24 * 1024 * 1024),
+        cost_estimate=pl.CostEstimate(
+            flops=12 * order_count * cycles * slots, bytes_accessed=20_000_000, transcendentals=0
+        ),
+        name="recursion",
+    )(ratio_main, ratio_back, starting, cosine, weight, jnp.broadcast_to(order_value, (order_count, slots)))
+
+
+def dot32(left, right):
+    return jnp.dot(left, right, preferred_element_type=jnp.float32)
+
+
+def turned_dot(left, right):
+    return lax.dot_general(
+        left, right, (((0,), (0,)), ((), ())), preferred_element_type=jnp.float32
+    )
+
+
+def value_kernel(cells, mask_ref, x_ref, own_ref, far_ref, inv_own_ref, inv_far_ref, expand_ref,
+                 contract_ref, out_ref):
+    base = pl.program_id(0) * cells
+    for cell in range(cells):
+        mixed = (
+            x_ref[cell].astype(jnp.float32)
+            + dot32(inv_own_ref[...], own_ref[cell])
+            + dot32(inv_far_ref[...], far_ref[cell])
+        )
+        hidden = gelu_value(dot32(mixed.astype(jnp.bfloat16), expand_ref[...])).astype(jnp.bfloat16)
+        result = mixed + dot32(hidden, contract_ref[...])
+        out_ref[cell] = (result * mask_ref[base + cell]).astype(jnp.bfloat16)
+
+
+def slope_kernel(cells, mask_ref, x_ref, grad_ref, own_ref, far_ref, inv_own_ref, inv_far_ref,
+                 turn_own_ref, turn_far_ref, expand_ref, expand_t_ref, contract_t_ref,
+                 mixed_out, own_out, far_out, sums_ref,
+                 mixed_all, masked_all, hidden_all, pre_all):
+    base = pl.program_id(0) * cells
+    points = x_ref.shape[1]
+
+    @pl.when(pl.program_id(0) == 0)
+    def _():
+        sums_ref[...] = jnp.zeros_like(sums_ref)
+
+    for cell in range(cells):
+        rows = pl.ds(cell * points, points)
+        mixed = (
+            x_ref[cell].astype(jnp.float32)
+            + dot32(inv_own_ref[...], own_ref[cell])
+            + dot32(inv_far_ref[...], far_ref[cell])
+        )
+        mixed_b = mixed.astype(jnp.bfloat16)
+        mixed_all[rows, :] = mixed_b
+        pre_act = dot32(mixed_b, expand_ref[...])
+        both = 0.5 * (1.0 + lax.erf(pre_act * ROOT_HALF))
+        hidden_all[rows, :] = (pre_act * both).astype(jnp.bfloat16)
+        slope = both + pre_act * jnp.exp(-0.5 * pre_act * pre_act) * INV_ROOT_TAU
+        masked = grad_ref[cell].astype(jnp.float32) * mask_ref[base + cell]
+        masked_b = masked.astype(jnp.bfloat16)
+        masked_all[rows, :] = masked_b
+        grad_pre = (dot32(masked_b, contract_t_ref[...]) * slope).astype(jnp.bfloat16)
+        pre_all[rows, :] = grad_pre
+        grad_mixed = (masked + dot32(grad_pre, expand_t_ref[...])).astype(jnp.bfloat16)
+        mixed_out[cell] = grad_mixed
+        own_out[cell] = dot32(turn_own_ref[...], grad_mixed).astype(jnp.bfloat16)
+        far_out[cell] = dot32(turn_far_ref[...], grad_mixed).astype(jnp.bfloat16)
+    sums_ref[0] += turned_dot(mixed_all[...], pre_all[...])
+    sums_ref[1] += turned_dot(masked_all[...], hidden_all[...])
+
+
+def row_spec(cells, array):
+    return pl.BlockSpec((cells,) + array.shape[1:], lambda at: (at,) + (0,) * (array.ndim - 1))
+
+
+def whole_spec(array):
+    return pl.BlockSpec(array.shape, lambda at: (0,) * array.ndim)
+
+
+def cells_at_once(row_count, most):
+    return max(c for c in range(1, most + 1) if row_count % c == 0)
+
+
+def value_rows(mask, x, own, far, inv_own, inv_far, expand, contract):
+    cells = cells_at_once(x.shape[0], 2)
+    work = 4 * x.shape[0] * x.shape[1] * expand.size
+    return pl.pallas_call(
+        functools.partial(value_kernel, cells),
+        grid=(x.shape[0] // cells,),
+        out_shape=jax.ShapeDtypeStruct(x.shape, jnp.bfloat16),
+        in_specs=[pl.BlockSpec(memory_space=pltpu.SMEM)]
+        + [row_spec(cells, a) for a in (x, own, far)]
+        + [whole_spec(a) for a in (inv_own, inv_far, expand, contract)],
+        out_specs=row_spec(cells, x),
+        compiler_params=pltpu.CompilerParams(vmem_limit_bytes=VMEM_BYTES),
+        cost_estimate=pl.CostEstimate(flops=5 * work, bytes_accessed=8 * x.size, transcendentals=0),
+        name="value_rows",
+    )(mask, x, own, far, inv_own, inv_far, expand, contract)
+
+
+def slope_rows(mask, x, grad, own, far, inv_own, inv_far, expand, contract):
+    cells = cells_at_once(x.shape[0], 2)
+    points, chan = x.shape[1:]
+    hid = expand.shape[1]
+    work = 10 * x.shape[0] * points * expand.size
+    rows = [x, grad, own, far]
+    whole = [inv_own, inv_far, inv_own.T, inv_far.T, expand, expand.T, contract.T]
+    sums = jax.ShapeDtypeStruct((2, chan, hid), jnp.float32)
+    return pl.pallas_call(
+        functools.partial(slope_kernel, cells),
+        grid=(x.shape[0] // cells,),
+        out_shape=[jax.ShapeDtypeStruct(a.shape, jnp.bfloat16) for a in (x, own, far)] + [sums],
+        in_specs=[pl.BlockSpec(memory_space=pltpu.SMEM)]
+        + [row_spec(cells, a) for a in rows]
+        + [whole_spec(a) for a in whole],
+        out_specs=[row_spec(cells, a) for a in (x, own, far)] + [whole_spec(sums)],
+        scratch_shapes=[
+            pltpu.VMEM((cells * points, chan), jnp.bfloat16),
+            pltpu.VMEM((cells * points, chan), jnp.bfloat16),
+            pltpu.VMEM((cells * points, hid), jnp.bfloat16),
+            pltpu.VMEM((cells * points, hid), jnp.bfloat16),
+        ],
+        compiler_params=pltpu.CompilerParams(vmem_limit_bytes=VMEM_BYTES),
+        cost_estimate=pl.CostEstimate(flops=4 * work, bytes_accessed=12 * x.size, transcendentals=0),
+        name="slope_rows",
+    )(mask, *rows, *whole)
+
+
+def swap(block, axis, mask=1):
+    return lax.ppermute(block, axis, [(i, i ^ mask) for i in range(lax.axis_size(axis))])
+
+
+def pair_sum(block, axis):
+    mask = 1
+    while mask < lax.axis_size(axis):
+        block = block + swap(block, axis, mask)
+        mask *= 2
+    return block
+
+
+def scatter_sum(block, axis):
+    mask = lax.axis_size(axis) // 2
+    place = lax.axis_index(axis)
+    while mask:
+        low, high = jnp.split(block, 2, axis=-1)
+        upper = (place & mask) != 0
+        kept = jnp.where(upper, high, low).astype(jnp.float32)
+        sent = jnp.where(upper, low, high).astype(jnp.bfloat16)
+        block = kept + swap(sent, axis, mask).astype(jnp.float32)
+        mask //= 2
+    return block
+
+
+def paired_on_device(
+    fresh_input, saved_input, output_grad, expand_weight, reduce_weight, filter_weight, cycle_table
+):
+    slot_count = fresh_input.shape[2]
+    position = lax.axis_index("sp")
+    order_table = jnp.arange(slot_count * 2, dtype=jnp.int32)
+    here, there = position * slot_count, (1 - position) * slot_count
+    cut = functools.partial(lax.dynamic_slice_in_dim, slice_size=slot_count)
+    own_cycles, far_cycles = cut(cycle_table, here), cut(cycle_table, there)
+    own_orders, far_orders = cut(order_table, here), cut(order_table, there)
+    cycle_mask = (own_cycles < NLAT).astype(jnp.float32)
+    forward_own, inverse_own = fourier_tables(own_orders, NLAT, NLON)
+    forward_far, inverse_far = fourier_tables(far_orders, NLAT, NLON)
+    forward_own = interleave(forward_own, slot_count)
+    forward_far = interleave(forward_far, slot_count)
+    inverse_own = interleave(inverse_own.T, slot_count)
+    inverse_far = interleave(inverse_far.T, slot_count)
+    filt = filter_weight[0]
+    expand = expand_weight[0]
+    contract = reduce_weight[0]
+    fresh = fresh_input[0, 0]
+    saved = saved_input[0, 0]
+    points, chan_count = fresh.shape[1:]
+
+    def longitude(x, table):
+        return jnp.einsum(
+            "jnc,nk->jkc", x, table, preferred_element_type=jnp.float32
+        ).astype(jnp.bfloat16)
+
+    saved_far = swap(longitude(saved, forward_far), "sp")
+    saved_own = longitude(saved, forward_own)
+    fresh_send = longitude(fresh, forward_far)
+    fresh_own = longitude(fresh, forward_own)
+    analysis, synthesis = legendre_tables(
+        jnp.concatenate([own_cycles, far_cycles]), own_orders, NLAT
+    )
+
+    def to_degrees(own, far, table):
+        both = jnp.concatenate([own, far], axis=0)
+        both = both.reshape(2 * slot_count, slot_count, 2, chan_count)
+        return jnp.einsum("tlj,jtrc->trlc", table, both, preferred_element_type=jnp.float32)
+
+    def to_rows(spectra, table):
+        rows = jnp.einsum(
+            "tlj,trlc->jtrc", table, spectra, preferred_element_type=jnp.float32
+        ).astype(jnp.bfloat16)
+        rows = rows.reshape(2 * slot_count, 2 * slot_count, chan_count)
+        return rows[:slot_count], rows[slot_count:]
+
+    def filtered(spectra):
+        real_part = filt[0] * spectra[:, 0] - filt[1] * spectra[:, 1]
+        imag_part = filt[0] * spectra[:, 1] + filt[1] * spectra[:, 0]
+        return jnp.stack([real_part, imag_part], axis=1).astype(jnp.bfloat16)
+
+    spectra = to_degrees(saved_own, saved_far, analysis)
+    own_values, far_values = to_rows(filtered(spectra), synthesis)
+    came_values = swap(far_values, "sp")
+    fresh_far = swap(fresh_send, "sp")
+    fresh_filtered = filtered(to_degrees(fresh_own, fresh_far, analysis))
+    fresh_own_values, fresh_far_values = to_rows(fresh_filtered, synthesis)
+    fresh_came = swap(fresh_far_values, "sp")
+
+    grad_mixed, grad_own, grad_send, sums = slope_rows(
+        cycle_mask, saved, output_grad[0, 0], own_values, came_values, inverse_own, inverse_far,
+        expand, contract,
+    )
+    grad_far = swap(grad_send, "sp")
+    block = value_rows(
+        cycle_mask, fresh, fresh_own_values, fresh_came, inverse_own, inverse_far, expand, contract
+    )
+    next_input = from_behind(block[None, None], "pipe", 1)
+    grad_filtered = to_degrees(grad_own, grad_far, synthesis)
+    filter_real = jnp.sum(
+        grad_filtered[:, 0] * spectra[:, 0] + grad_filtered[:, 1] * spectra[:, 1], axis=0
+    )
+    filter_imag = jnp.sum(
+        grad_filtered[:, 1] * spectra[:, 0] - grad_filtered[:, 0] * spectra[:, 1], axis=0
+    )
+    grad_spectra = jnp.stack(
+        [
+            filt[0] * grad_filtered[:, 0] + filt[1] * grad_filtered[:, 1],
+            filt[0] * grad_filtered[:, 1] - filt[1] * grad_filtered[:, 0],
+        ],
+        axis=1,
+    ).astype(jnp.bfloat16)
+    own_coeffs, far_coeffs = to_rows(grad_spectra, analysis)
+    came_coeffs = swap(far_coeffs, "sp")
+    filter_grad = pair_sum(pair_sum(jnp.stack([filter_real, filter_imag]), "sp"), "dp")
+    sums = sums + swap(sums.astype(jnp.bfloat16), "sp").astype(jnp.float32)
+    sums = scatter_sum(sums, "dp")
+    grad_tokens = jnp.einsum(
+        "jkc,nk->jnc", own_coeffs, forward_own, preferred_element_type=jnp.float32
+    ) + jnp.einsum("jkc,nk->jnc", came_coeffs, forward_far, preferred_element_type=jnp.float32)
+    input_grad = (
+        (grad_mixed.astype(jnp.float32) + grad_tokens) * cycle_mask[:, None, None]
+    ).astype(jnp.bfloat16)
+    sent_back = from_behind(input_grad[None, None], "pipe", -1)
+    return (next_input, sent_back, sums[0][None], sums[1].T[None], filter_grad[None])
+
+
 def solution(mesh):
+    groups = mesh.shape["dp"]
+    paired = mesh.shape["sp"] == 2 and groups & (groups - 1) == 0
     return jax.shard_map(
-        on_device,
+        paired_on_device if paired else on_device,
         mesh=mesh,
         in_specs=(
             P("pipe", "dp", "sp", None, None),

time: 813 us -> 373 us (0.46)
  other arithmetic: 146 us -> 16.5 us
  matrix products: 161 us -> 35.9 us
  local copies, waits for them, and re-layouts: 153 us -> 37.8 us
  Pallas kernels: 0 us -> 102 us
  loops' own time: 80.9 us -> 0 us
  waiting for transfers between devices: 214 us -> 144 us
  between operations: 15.8 us -> 1.35 us
    ppermute x0 -> x12, waiting for transfers between devices: none -> 139 us  [swap(): lax.ppermute(block, axis, [(i, i ^ mask) for i in range(lax.axis_size(axi...]
    dot_general x14 -> x12, matrix products: 161 us -> 35.9 us  [the longest x4 11.8 us: longitude(): jnp.einsum('jnc,nk->jkc', x, table, preferred_element_type=jnp.float32)]
    all_to_all x4 -> x0, waiting for transfers between devices: 105 us -> none  [the longest x1 65.8 us: joint_cycles(): return lax.all_to_all(values, 'sp', split_axis=1, concat_axis=3, tiled=True)]
    pallas_call x0 -> x3, Pallas kernels: none -> 102 us  [the longest x1 60.8 us: slope_rows(): pl.pallas_call(functools.partial(slope_kernel, cells), grid=(x.shape[0] /...]
    psum x2 -> x0, waiting for transfers between devices: 90.5 us -> none  [the longest x1 66.9 us: on_device(): filter_grad = lax.psum(jnp.stack([filter_real, filter_imag]), ('sp', 'dp'))]
    dynamic_update_slice x120 -> x0, other arithmetic: 87.6 us -> none  [legendre(): lax.scan(advance, (zero_rows, zero_rows), jnp.arange(cycles, dtype=jnp.in...]
    another operation x1 -> x0, loops' own time: 80.9 us -> none  [legendre(): lax.scan(advance, (zero_rows, zero_rows), jnp.arange(cycles, dtype=jnp.in...]
    dynamic_slice x120 -> x1, local copies, waits for them, and re-layouts: 69.9 us -> 0.07 us  [paired_on_device(): own_cycles, far_cycles = (cut(cycle_table, here), cut(cycle_table, there))]
  transfers between devices with their start and end apart: 10 -> 14, of which waited for: 6 -> 10; matrix products, arithmetic and copies ran while one was open for 35% -> 12% of each run, Pallas kernels for 0% -> 28%
where the time goes in v1:
time: 373 us; the launch traced here: 368 us
  waiting for transfers between devices  144 us (39%)
  Pallas kernels  102 us (27%)
  local copies, waits for them, and re-layouts  37.8 us (10%)
  matrix products  35.9 us (10%)
  starting transfers between devices  30.9 us (8%)
  other arithmetic  16.5 us (4%)
    ppermute x12, waiting for transfers between devices, swap(): lax.ppermute(block, axis, [(i, i ^ mask) for i in range(lax.axis_size(axi...  139 us
    pallas_call x1, Pallas kernels, slope_rows(): pl.pallas_call(functools.partial(slope_kernel, cells), grid=(x.shape[0] /...  60.8 us
    pallas_call x1, Pallas kernels, value_rows(): pl.pallas_call(functools.partial(value_kernel, cells), grid=(x.shape[0] /...  36.6 us
    slice x8, local copies, waits for them, and re-layouts, to_rows(): return (rows[:slot_count], rows[slot_count:])  20.5 us
    ppermute x2, starting transfers between devices, from_behind(): return lax.ppermute(block, axis, route)  15.7 us
    ppermute x12, starting transfers between devices, swap(): lax.ppermute(block, axis, [(i, i ^ mask) for i in range(lax.axis_size(axi...  15.2 us
    unnamed x42, local copies, waits for them, and re-layouts  15 us
    dot_general x4, matrix products, longitude(): jnp.einsum('jnc,nk->jkc', x, table, preferred_element_type=jnp.float32)  11.8 us
  transfers between devices with their start and end apart: 14, of which 10 were waited for; matrix products, arithmetic and copies ran while one was open for 12% of the time, Pallas kernels for 28%

profile of v1, /device:TPU:1, one launch (start us, length us, event | category | flops | bytes accessed | tf_op | source)
XLA Modules:
  0.0 368.4 jit_solution(15485464306882912035)
XLA Ops:
  0.8 0.4 multiply_convert_fusion.1
  1.4 3.9 %convert_bitcast_fusion.3 = bf16[60,120,128]{2,1,0:T(8,128)(2,1)} fusion(bf16[240,120,1]{0,1,2:T(8,128)(2,1)S(1)} %reshape.579, bf16[1,1,60,240,128]{4,3,2,1,0:T(8,128)(2,1)} %param.8), kind=kOutput, calls=%fused_computation.48 | convolution fusion | flops 443289600 | bytes 5587200 | tf_op jit(solution)/shard_map/jnc,nk->jkc/dot_general | solution.py:492
  5.3 2.1 collective-permute-start.3
  7.5 0.4 multiply_convert_fusion.3
  8.3 0.7 compare_convert_fusion.1
  9.4 4.2 %recursion.1 = (bf16[60,120,120]{2,1,0:T(8,128)(2,1)S(1)}, bf16[60,120,120]{2,1,0:T(8,128)(2,1)S(1)}) custom-call(f32[60,120]{1,0:T(8,128)S(1)} %get-tuple-element.70.main_ref, f32[60,120]{1,0:T(8,128)S(1)} %get-tuple-element.69.back_ref, f32[60,120]{1,0:T(8,128)S(1)} %get-tuple-element.73.start_ref, f32[1,120]{1,0:T(1,128)S(1)} %get-tuple-element.53.cos_ref, ...), custom_call_target="tpu_custom_call" | custom-call | flops 10368000 | bytes 20000000 | tf_op jit(solution)/shard_map/recursion/pallas_call | solution.py:310
  13.7 3.3 convert_bitcast_fusion.4
  17.1 30.5 %collective-permute-done.3 = bf16[60,120,128]{2,1,0:T(8,128)(2,1)} collective-permute-done((bf16[60,120,128]{2,1,0:T(8,128)(2,1)}, bf16[60,120,128]{2,1,0:T(8,128)(2,1)}, u32[]{:S(2)}, u32[]{:S(2)}) %collective-permute-start.3) | collective-permute-done | bytes 1843232 | tf_op jit(solution)/shard_map/ppermute | solution.py:443
  47.5 1.8 pad_maximum_fusion.1
  49.4 1.1 fusion.24
  50.5 1.0 subtract_convert_fusion.1
  51.5 1.9 copy-done.2
  53.4 1.3 convert_bitcast_fusion.1
  54.7 2.1 fusion.84
  56.8 3.1 copy.29
  60.0 1.2 collective-permute-start.4
  61.1 1.9 convert_bitcast_fusion.5
  63.4 0.7 copy.23.inv_far_ref
  64.3 0.7 copy.22.inv_own_ref
  65.0 0.8 copy.20
  65.9 0.8 copy.21
  66.7 4.7 %copy.28 = bf16[60,60,2,128]{3,2,1,0:T(2,128)(2,1)} copy(bf16[60,60,2,128]{3,0,2,1:T(8,128)(2,1)} %get-tuple-element.39) | data formatting | bytes 3686400 | tf_op jit(solution)/shard_map/slice | solution.py:514
  71.4 29.4 %collective-permute-done.4.far_ref = bf16[60,120,128]{2,1,0:T(8,128)(2,1)} collective-permute-done((bf16[60,120,128]{2,1,0:T(8,128)(2,1)}, bf16[60,120,128]{2,1,0:T(8,128)(2,1)}, u32[]{:S(2)}, u32[]{:S(2)}) %collective-permute-start.4) | collective-permute-done | bytes 1843232 | tf_op jit(solution)/shard_map/ppermute | solution.py:443
  100.8 60.8 %slope_rows.1 = (bf16[60,240,128]{2,1,0:T(8,128)(2,1)}, bf16[60,120,128]{2,1,0:T(8,128)(2,1)}, bf16[60,120,128]{2,1,0:T(8,128)(2,1)}, f32[2,128,768]{2,1,0:T(8,128)}) custom-call(f32[60]{0:T(128)} %get-tuple-element.26.mask_ref, bf16[60,240,128]{2,1,0:T(8,128)(2,1)} %bitcast.142, bf16[60,240,128]{2,1,0:T(8,128)(2,1)} %bitcast.164, ...), custom_call_target="tpu_custom_call" | custom-call | flops 56623104000 | bytes 22118400 | tf_op jit(solution)/shard_map/slope_rows/pallas_call | solution.py:422
  161.6 1.0 collective-permute-start.5
  162.6 2.7 convert_bitcast_fusion.6
  165.3 1.8 pad_maximum_fusion
  167.1 1.1 fusion.21
  168.2 31.6 %collective-permute-done.5 = bf16[60,120,128]{2,1,0:T(8,128)(2,1)S(1)} collective-permute-done((bf16[60,120,128]{2,1,0:T(8,128)(2,1)}, bf16[60,120,128]{2,1,0:T(8,128)(2,1)S(1)}, u32[]{:S(2)}, u32[]{:S(2)}) %collective-permute-start.5) | collective-permute-done | bytes 1843232 | tf_op jit(solution)/shard_map/ppermute | solution.py:443
  199.8 1.2 copy-done.8
  201.1 2.0 pad_maximum_fusion.2
  203.1 4.1 %fusion.27 = f32[60,2,120,128]{3,2,1,0:T(8,128)} fusion(bf16[120,60,2,128]{3,2,1,0:T(2,128)(2,1)S(1)} %bitcast.146, bf16[60,120,120]{2,1,0:T(8,128)(2,1)S(1)} %copy-done.1), kind=kOutput, calls=%fused_computation.39 | convolution fusion | flops 442368000 | bytes 12787200 | tf_op jit(solution)/shard_map/tlj,jtrc->trlc/dot_general | solution.py:507
  207.3 6.6 %add_reduce_fusion = (f32[120,128]{1,0:T(8,128)S(1)}, f32[120,128]{1,0:T(8,128)S(1)}, bf16[60,1,120,128]{3,2,1,0:T(8,128)(2,1)}, bf16[60,1,120,128]{3,2,1,0:T(8,...) fusion(f32[60,2,120,128]{3,2,1,0:T(8,128)} %fusion.27, ...), kind=kLoop, calls=%fused_computation.27 | loop fusion | flops 22087680 | bytes 29736960 | tf_op jit(solution)/shard_map/reduce_sum | solution.py:539
  213.8 1.3 convert_bitcast_fusion.2
  215.2 2.1 fusion.85
  217.3 3.2 copy.17
  220.9 3.3 convert_bitcast_fusion
  224.2 1.0 fusion.83
  225.2 1.2 copy.36
  226.7 3.1 copy.16
  229.9 1.1 collective-permute-start.6
  231.0 4.5 %fusion.36 = f32[240,60,128,1]{2,0,3,1:T(8,128)} fusion(bf16[60,60,2,128]{3,0,2,1:T(8,128)(2,1)S(1)} %get-tuple-element.37, bf16[240,1,60]{0,2,1:T(8,128)(2,1)S(1)} %get-tuple-element.62, bf16[240,1,60]{0,2,1:T(8,128)(2,1)S(1)} %get-tuple-element.63), kind=kOutput, calls=%fused_computation.40 | convolution fusion | flops 442483200 | bytes 9273600 | tf_op jit(solution)/shard_map/jkc,nk->jnc/dot_general | solution.py:557
  235.5 22.4 %collective-permute-done.1.far_ref = bf16[60,120,128]{2,1,0:T(8,128)(2,1)} collective-permute-done((bf16[60,120,128]{2,1,0:T(8,128)(2,1)}, bf16[60,120,128]{2,1,0:T(8,128)(2,1)}, u32[]{:S(2)}, u32[]{:S(2)}) %collective-permute-start.1) | collective-permute-done | bytes 1843232 | tf_op jit(solution)/shard_map/ppermute | solution.py:443
  257.9 36.6 %value_rows.1 = bf16[60,240,128]{2,1,0:T(8,128)(2,1)} custom-call(f32[60]{0:T(128)} %get-tuple-element.26.mask_ref, bf16[60,240,128]{2,1,0:T(8,128)(2,1)} %bitcast.143, bf16[60,120,128]{2,1,0:T(8,128)(2,1)} %bitcast.148, bf16[60,120,128]{2,1,0:T(8,128)(2,1)} %collective-permute-done.1.far_ref, bf16[240,120]{1,0:T(8,128)(2,1)} %copy.22.inv_own_ref, ...), custom_call_target="tpu_custom_call" | custom-call | flops 28311552000 | bytes 14745600 | tf_op jit(solution)/shard_map/value_rows/pallas_call | solution.py:400
  294.5 13.3 %collective-permute-start.2 = (bf16[1,1,60,240,128]{4,3,2,1,0:T(8,128)(2,1)}, bf16[1,1,60,240,128]{4,3,2,1,0:T(8,128)(2,1)}, u32[]{:S(2)}, u32[]{:S(2)}) collective-permute-start(bf16[1,1,60,240,128]{4,3,2,1,0:T(8,128)(2,1)} %bitcast.165), channel_id=1, source_target_pairs={{0,8},{8,16},{16,24},{1,9},{9,17},{17,25},{2,10},{10,18},{18,26},{... | collective-permute-start | bytes 11059208 | tf_op jit(solution)/shard_map/ppermute | solution.py:22
  307.9 7.3 %fusion.2 = bf16[1,1,60,240,128]{4,3,2,1,0:T(8,128)(2,1)} fusion(f32[240,60,128,1]{2,0,3,1:T(8,128)} %fusion.36, bf16[60,240,128]{2,1,0:T(8,128)(2,1)S(1)} %copy-done.5, f32[60]{0:T(128)S(1)} %copy-done.14, bf16[60,120,128]{2,1,0:T(8,128)(2,1)} %collective-permute-done.6, bf16[240,120]{0,1:T(8,128)(2,1)S(1)} %reshape.572), kind=kOutput, calls=%fused_computation.4 | convolution fusion | flops 451584000 | bytes 16646640 | tf_op jit(solution)/shard_map/jkc,nk->jnc/dot_general | solution.py:559
  315.2 2.4 collective-permute-start.7
  317.6 1.0 collective-permute-start.8
  318.6 9.9 %collective-permute-done.8 = bf16[2,128,768]{2,1,0:T(8,128)(2,1)S(1)} collective-permute-done((bf16[2,128,768]{2,1,0:T(8,128)(2,1)S(1)}, bf16[2,128,768]{2,1,0:T(8,128)(2,1)S(1)}, u32[]{:S(2)}, u32[]{:S(2)}) %collective-permute-start.8) | collective-permute-done | bytes 393248 | tf_op jit(solution)/shard_map/ppermute | solution.py:443
  328.6 2.0 collective-permute-start.9
  330.7 9.3 %collective-permute-done.9 = bf16[2,128,384]{2,1,0:T(8,128)(2,1)S(1)} collective-permute-done((bf16[2,128,384]{2,1,0:T(8,128)(2,1)S(1)}, bf16[2,128,384]{2,1,0:T(8,128)(2,1)S(1)}, u32[]{:S(2)}, u32[]{:S(2)}) %collective-permute-start.9) | collective-permute-done | bytes 196640 | tf_op jit(solution)/shard_map/ppermute | solution.py:443
  340.0 0.9 collective-permute-start.11
  341.0 1.2 collective-permute-start.10
  342.3 1.5 collective-permute-done.11
  343.8 1.5 collective-permute-start.12
  345.5 2.8 collective-permute-done.12
  348.3 2.5 collective-permute-start.13
  350.8 0.7 copy.39
  351.6 0.7 copy.38
  352.3 2.1 collective-permute-done.13
  354.4 0.7 add_bitcast_fusion
  355.1 4.8 %collective-permute-done.7 = bf16[1,1,60,240,128]{4,3,2,1,0:T(8,128)(2,1)} collective-permute-done((bf16[1,1,60,240,128]{4,3,2,1,0:T(8,128)(2,1)}, bf16[1,1,60,240,128]{4,3,2,1,0:T(8,128)(2,1)}, u32[]{:S(2)}, u32[]{:S(2)}) %collective-permute-start.7) | collective-permute-done | bytes 3686432 | tf_op jit(solution)/shard_map/ppermute | solution.py:22
  359.9 4.1 %copy.73 = bf16[1,1,60,240,128]{4,3,2,1,0:T(8,128)(2,1)} copy(bf16[1,1,60,240,128]{4,3,2,1,0:T(8,128)(2,1)} %collective-permute-done.2) | data formatting | bytes 7372800
  364.0 4.1 %copy.74 = bf16[1,1,60,240,128]{4,3,2,1,0:T(8,128)(2,1)} copy(bf16[1,1,60,240,128]{4,3,2,1,0:T(8,128)(2,1)} %collective-permute-done.7) | data formatting | bytes 7372800
  (82 shorter events, 3.3 us)
Async XLA Ops:
  0.6 7.3 %copy-start.15 = (s32[120]{0:T(128)S(1)}, s32[120]{0:T(128)}, u32[]{:S(2)}) copy-start(s32[120]{0:T(128)} %param.13) | copy-start | bytes 1444
  0.6 13.0 %copy-start.13 = (f32[1,2,120,128]{3,2,1,0:T(8,128)S(1)}, f32[1,2,120,128]{3,2,1,0:T(8,128)}, u32[]{:S(2)}) copy-start(f32[1,2,120,128]{3,2,1,0:T(8,128)} %param.12) | copy-start | bytes 368644
  5.3 42.3 %collective-permute-start.3 = (bf16[60,120,128]{2,1,0:T(8,128)(2,1)}, bf16[60,120,128]{2,1,0:T(8,128)(2,1)}, u32[]{:S(2)}, u32[]{:S(2)}) collective-permute-start(bf16[60,120,128]{2,1,0:T(8,128)(2,1)} %convert_bitcast_fusion.3), channel_id=1, source_target_pairs={{0,4},{4,0},{1,5},{5,1},{2,6},{6,2},{3,7},{7,3},{8,12},{12,8},{9,1... | collective-permute-start | bytes 5529608 | tf_op jit(solution)/shard_map/ppermute | solution.py:443
  13.7 39.7 %copy-start = (bf16[60,120,120]{2,1,0:T(8,128)(2,1)}, bf16[60,120,120]{2,1,0:T(8,128)(2,1)S(1)}, u32[]{:S(2)}) copy-start(bf16[60,120,120]{2,1,0:T(8,128)(2,1)S(1)} %get-tuple-element.12) | copy-start | bytes 5184004
  50.5 2.9 copy-start.2
  56.8 4.3 %copy-start.3 = (bf16[1,1,60,240,128]{4,3,2,1,0:T(8,128)(2,1)S(1)}, bf16[1,1,60,240,128]{4,3,2,1,0:T(8,128)(2,1)}, u32[]{:S(2)}) copy-start(bf16[1,1,60,240,128]{4,3,2,1,0:T(8,128)(2,1)} %param.7) | copy-start | bytes 11059204
  59.9 5.1 %copy-start.11 = (bf16[1,128,768]{2,1,0:T(8,128)(2,1)S(1)}, bf16[1,128,768]{2,1,0:T(8,128)(2,1)}, u32[]{:S(2)}) copy-start(bf16[1,128,768]{2,1,0:T(8,128)(2,1)} %param.10) | copy-start | bytes 589828
  59.9 5.9 %copy-start.12 = (bf16[1,768,128]{2,1,0:T(8,128)(2,1)S(1)}, bf16[1,768,128]{2,1,0:T(8,128)(2,1)}, u32[]{:S(2)}) copy-start(bf16[1,768,128]{2,1,0:T(8,128)(2,1)} %param.11) | copy-start | bytes 589828
  60.0 40.8 %collective-permute-start.4 = (bf16[60,120,128]{2,1,0:T(8,128)(2,1)}, bf16[60,120,128]{2,1,0:T(8,128)(2,1)}, u32[]{:S(2)}, u32[]{:S(2)}) collective-permute-start(bf16[60,120,128]{2,1,0:T(8,128)(2,1)} %bitcast.34), channel_id=1, source_target_pairs={{0,4},{4,0},{1,5},{5,1},{2,6},{6,2},{3,7},{7,3},{8,12},{12,8},{9,1... | collective-permute-start | bytes 5529608 | tf_op jit(solution)/shard_map/ppermute | solution.py:443
  63.0 102.2 %collective-permute-start = (bf16[60,120,128]{2,1,0:T(8,128)(2,1)}, bf16[60,120,128]{2,1,0:T(8,128)(2,1)}, u32[]{:S(2)}, u32[]{:S(2)}) collective-permute-start(bf16[60,120,128]{2,1,0:T(8,128)(2,1)} %convert_bitcast_fusion.5), channel_id=1, source_target_pairs={{0,4},{4,0},{1,5},{5,1},{2,6},{6,2},{3,7},{7,3},{8,12},{12,8},{9,1... | collective-permute-start | bytes 5529608 | tf_op jit(solution)/shard_map/ppermute | solution.py:443
  63.4 37.3 %copy-start.9 = (bf16[240,120]{0,1:T(8,128)(2,1)}, bf16[240,120]{0,1:T(8,128)(2,1)S(1)}, u32[]{:S(2)}) copy-start(bf16[240,120]{0,1:T(8,128)(2,1)S(1)} %reshape.575) | copy-start | bytes 172804
  64.3 36.5 %copy-start.10 = (bf16[240,120]{0,1:T(8,128)(2,1)}, bf16[240,120]{0,1:T(8,128)(2,1)S(1)}, u32[]{:S(2)}) copy-start(bf16[240,120]{0,1:T(8,128)(2,1)S(1)} %reshape.574) | copy-start | bytes 172804
  161.6 38.2 %collective-permute-start.5 = (bf16[60,120,128]{2,1,0:T(8,128)(2,1)}, bf16[60,120,128]{2,1,0:T(8,128)(2,1)S(1)}, u32[]{:S(2)}, u32[]{:S(2)}) collective-permute-start(bf16[60,120,128]{2,1,0:T(8,128)(2,1)} %get-tuple-element.15), channel_id=1, source_target_pairs={{0,4},{4,0},{1,5},{5,1},{2,6},{6,2},{3,7},{7,3},{8,12},{12,8},{9,1... | collective-permute-start | bytes 5529608 | tf_op jit(solution)/shard_map/ppermute | solution.py:443
  167.1 33.9 %copy-start.7 = (bf16[60,120,128]{2,1,0:T(8,128)(2,1)S(1)}, bf16[60,120,128]{2,1,0:T(8,128)(2,1)}, u32[]{:S(2)}) copy-start(bf16[60,120,128]{2,1,0:T(8,128)(2,1)} %get-tuple-element.14) | copy-start | bytes 5529604
  199.8 1.2 copy-start.8
  201.0 2.1 copy-start.1
  201.0 6.2 %slice-start = ((s8[7372800]{0:T(1024)(128)(4,1)}), s8[4194304]{0:T(1024)(128)(4,1)S(1)}, s32[]{:S(2)}) async-start(s8[7372800]{0:T(1024)(128)(4,1)} %bitcast.140), calls=%async_computation | async-start | bytes 8388608
  203.1 4.1 %slice-start.1 = ((s8[7372800]{0:T(1024)(128)(4,1)}), s8[3178496]{0:T(1024)(128)(4,1)S(1)}, s32[]{:S(2)}) async-start(s8[7372800]{0:T(1024)(128)(4,1)} %bitcast.140), calls=%async_computation.1 | async-start | bytes 6356992
  220.5 37.4 %collective-permute-start.1 = (bf16[60,120,128]{2,1,0:T(8,128)(2,1)}, bf16[60,120,128]{2,1,0:T(8,128)(2,1)}, u32[]{:S(2)}, u32[]{:S(2)}) collective-permute-start(bf16[60,120,128]{2,1,0:T(8,128)(2,1)} %bitcast.16), channel_id=1, source_target_pairs={{0,4},{4,0},{1,5},{5,1},{2,6},{6,2},{3,7},{7,3},{8,12},{12,8},{9,1... | collective-permute-start | bytes 5529608 | tf_op jit(solution)/shard_map/ppermute | solution.py:443
  225.2 1.5 copy-start.4
  229.9 78.0 %collective-permute-start.6 = (bf16[60,120,128]{2,1,0:T(8,128)(2,1)S(1)}, bf16[60,120,128]{2,1,0:T(8,128)(2,1)}, u32[]{:S(2)}, u32[]{:S(2)}) collective-permute-start(bf16[60,120,128]{2,1,0:T(8,128)(2,1)S(1)} %copy.36), channel_id=1, source_target_pairs={{0,4},{4,0},{1,5},{5,1},{2,6},{6,2},{3,7},{7,3},{8,12},{12,8},{9,1... | collective-permute-start | bytes 5529608 | tf_op jit(solution)/shard_map/ppermute | solution.py:443
  257.9 50.0 %copy-start.5 = (bf16[60,240,128]{2,1,0:T(8,128)(2,1)S(1)}, bf16[60,240,128]{2,1,0:T(8,128)(2,1)}, u32[]{:S(2)}) copy-start(bf16[60,240,128]{2,1,0:T(8,128)(2,1)} %get-tuple-element.13) | copy-start | bytes 11059204
  257.9 50.0 %copy-start.14 = (f32[60]{0:T(128)S(1)}, f32[60]{0:T(128)}, u32[]{:S(2)}) copy-start(f32[60]{0:T(128)} %get-tuple-element.26.mask_ref) | copy-start | bytes 724
  294.5 60.5 %collective-permute-start.2 = (bf16[1,1,60,240,128]{4,3,2,1,0:T(8,128)(2,1)}, bf16[1,1,60,240,128]{4,3,2,1,0:T(8,128)(2,1)}, u32[]{:S(2)}, u32[]{:S(2)}) collective-permute-start(bf16[1,1,60,240,128]{4,3,2,1,0:T(8,128)(2,1)} %bitcast.165), channel_id=1, source_target_pairs={{0,8},{8,16},{16,24},{1,9},{9,17},{17,25},{2,10},{10,18},{18,26},{... | collective-permute-start | bytes 11059208 | tf_op jit(solution)/shard_map/ppermute | solution.py:22
  307.9 9.7 %copy-start.6 = (f32[2,128,768]{2,1,0:T(8,128)S(1)}, f32[2,128,768]{2,1,0:T(8,128)}, u32[]{:S(2)}) copy-start(f32[2,128,768]{2,1,0:T(8,128)} %get-tuple-element.16) | copy-start | bytes 2359300
  315.2 44.7 %collective-permute-start.7 = (bf16[1,1,60,240,128]{4,3,2,1,0:T(8,128)(2,1)}, bf16[1,1,60,240,128]{4,3,2,1,0:T(8,128)(2,1)}, u32[]{:S(2)}, u32[]{:S(2)}) collective-permute-start(bf16[1,1,60,240,128]{4,3,2,1,0:T(8,128)(2,1)} %fusion.2), channel_id=1, source_target_pairs={{8,0},{16,8},{24,16},{9,1},{17,9},{25,17},{10,2},{18,10},{26,18},{... | collective-permute-start | bytes 11059208 | tf_op jit(solution)/shard_map/ppermute | solution.py:22
  317.6 10.9 %collective-permute-start.8 = (bf16[2,128,768]{2,1,0:T(8,128)(2,1)S(1)}, bf16[2,128,768]{2,1,0:T(8,128)(2,1)S(1)}, u32[]{:S(2)}, u32[]{:S(2)}) collective-permute-start(bf16[2,128,768]{2,1,0:T(8,128)(2,1)S(1)} %convert_element_type.172), channel_id=1, source_target_pairs={{0,4},{4,0},{1,5},{5,1},{2,6},{6,2},{3,7},{7,3},{8,12},{12,8},{9,1... | collective-permute-start | bytes 1179656 | tf_op jit(solution)/shard_map/ppermute | solution.py:443
  328.6 11.3 %collective-permute-start.9 = (bf16[2,128,384]{2,1,0:T(8,128)(2,1)S(1)}, bf16[2,128,384]{2,1,0:T(8,128)(2,1)S(1)}, u32[]{:S(2)}, u32[]{:S(2)}) collective-permute-start(bf16[2,128,384]{2,1,0:T(8,128)(2,1)S(1)} %select_convert_fusion), channel_id=1, source_target_pairs={{0,2},{1,3},{2,0},{3,1},{4,6},{5,7},{6,4},{7,5},{8,10},{9,11},{10,... | collective-permute-start | bytes 589832 | tf_op jit(solution)/shard_map/ppermute | solution.py:443
  340.0 3.8 %collective-permute-start.11 = (f32[2,120,128]{2,1,0:T(8,128)S(1)}, f32[2,120,128]{2,1,0:T(8,128)S(1)}, u32[]{:S(2)}, u32[]{:S(2)}) collective-permute-start(f32[2,120,128]{2,1,0:T(8,128)S(1)} %pad_maximum_fusion.3), channel_id=1, source_target_pairs={{0,4},{4,0},{1,5},{5,1},{2,6},{6,2},{3,7},{7,3},{8,12},{12,8},{9,1... | collective-permute-start | bytes 368648 | tf_op jit(solution)/shard_map/ppermute | solution.py:443
  341.0 4.3 %collective-permute-start.10 = (bf16[2,128,192]{2,1,0:T(8,128)(2,1)S(1)}, bf16[2,128,192]{2,1,0:T(8,128)(2,1)S(1)}, u32[]{:S(2)}, u32[]{:S(2)}) collective-permute-start(bf16[2,128,192]{2,1,0:T(8,128)(2,1)S(1)} %select_convert_fusion.1), channel_id=1, source_target_pairs={{0,1},{1,0},{2,3},{3,2},{4,5},{5,4},{6,7},{7,6},{8,9},{9,8},{10,11... | collective-permute-start | bytes 294920 | tf_op jit(solution)/shard_map/ppermute | solution.py:443
  343.8 4.4 %collective-permute-start.12 = (f32[2,120,128]{2,1,0:T(8,128)S(1)}, f32[2,120,128]{2,1,0:T(8,128)S(1)}, u32[]{:S(2)}, u32[]{:S(2)}) collective-permute-start(f32[2,120,128]{2,1,0:T(8,128)S(1)} %fusion.82), channel_id=1, source_target_pairs={{0,1},{1,0},{2,3},{3,2},{4,5},{5,4},{6,7},{7,6},{8,9},{9,8},{10,11... | collective-permute-start | bytes 368648 | tf_op jit(solution)/shard_map/ppermute | solution.py:443
  348.3 6.1 %collective-permute-start.13 = (f32[2,120,128]{2,1,0:T(8,128)S(1)}, f32[2,120,128]{2,1,0:T(8,128)S(1)}, u32[]{:S(2)}, u32[]{:S(2)}) collective-permute-start(f32[2,120,128]{2,1,0:T(8,128)S(1)} %fusion.91), channel_id=1, source_target_pairs={{0,2},{1,3},{2,0},{3,1},{4,6},{5,7},{6,4},{7,5},{8,10},{9,11},{10,... | collective-permute-start | bytes 368648 | tf_op jit(solution)/shard_map/ppermute | solution.py:443

commit v2 on v1

--- a/solution.py
+++ b/solution.py
@@ -331,9 +331,9 @@
     )
 
 
-def value_kernel(cells, mask_ref, x_ref, own_ref, far_ref, inv_own_ref, inv_far_ref, expand_ref,
+def value_kernel(cells, first, mask_ref, x_ref, own_ref, far_ref, inv_own_ref, inv_far_ref, expand_ref,
                  contract_ref, out_ref):
-    base = pl.program_id(0) * cells
+    base = first + pl.program_id(0) * cells
     for cell in range(cells):
         mixed = (
             x_ref[cell].astype(jnp.float32)
@@ -345,11 +345,11 @@
         out_ref[cell] = (result * mask_ref[base + cell]).astype(jnp.bfloat16)
 
 
-def slope_kernel(cells, mask_ref, x_ref, grad_ref, own_ref, far_ref, inv_own_ref, inv_far_ref,
+def slope_kernel(cells, first, mask_ref, x_ref, grad_ref, own_ref, far_ref, inv_own_ref, inv_far_ref,
                  turn_own_ref, turn_far_ref, expand_ref, expand_t_ref, contract_t_ref,
                  mixed_out, own_out, far_out, sums_ref,
                  mixed_all, masked_all, hidden_all, pre_all):
-    base = pl.program_id(0) * cells
+    base = first + pl.program_id(0) * cells
     points = x_ref.shape[1]
 
     @pl.when(pl.program_id(0) == 0)
@@ -382,8 +382,11 @@
     sums_ref[1] += turned_dot(masked_all[...], hidden_all[...])
 
 
-def row_spec(cells, array):
-    return pl.BlockSpec((cells,) + array.shape[1:], lambda at: (at,) + (0,) * (array.ndim - 1))
+def row_spec(cells, array, first=0):
+    skip = first // cells
+    return pl.BlockSpec(
+        (cells,) + array.shape[1:], lambda at: (at + skip,) + (0,) * (array.ndim - 1)
+    )
 
 
 def whole_spec(array):
@@ -394,39 +397,46 @@
     return max(c for c in range(1, most + 1) if row_count % c == 0)
 
 
-def value_rows(mask, x, own, far, inv_own, inv_far, expand, contract):
-    cells = cells_at_once(x.shape[0], 2)
-    work = 4 * x.shape[0] * x.shape[1] * expand.size
+def value_rows(mask, first, x, own, far, inv_own, inv_far, expand, contract):
+    count = far.shape[0]
+    cells = cells_at_once(math.gcd(count, first or count), 2)
+    points, chan = x.shape[1:]
+    out = jax.ShapeDtypeStruct((count, points, chan), jnp.bfloat16)
+    work = 4 * count * points * expand.size
     return pl.pallas_call(
-        functools.partial(value_kernel, cells),
-        grid=(x.shape[0] // cells,),
-        out_shape=jax.ShapeDtypeStruct(x.shape, jnp.bfloat16),
-        in_specs=[pl.BlockSpec(memory_space=pltpu.SMEM)]
-        + [row_spec(cells, a) for a in (x, own, far)]
+        functools.partial(value_kernel, cells, first),
+        grid=(count // cells,),
+        out_shape=out,
+        in_specs=[pl.BlockSpec(memory_space=pltpu.SMEM), row_spec(cells, x, first)]
+        + [row_spec(cells, a) for a in (own, far)]
         + [whole_spec(a) for a in (inv_own, inv_far, expand, contract)],
-        out_specs=row_spec(cells, x),
+        out_specs=row_spec(cells, out),
         compiler_params=pltpu.CompilerParams(vmem_limit_bytes=VMEM_BYTES),
-        cost_estimate=pl.CostEstimate(flops=5 * work, bytes_accessed=8 * x.size, transcendentals=0),
+        cost_estimate=pl.CostEstimate(
+            flops=2 * work, bytes_accessed=8 * count * points * chan, transcendentals=0
+        ),
         name="value_rows",
     )(mask, x, own, far, inv_own, inv_far, expand, contract)
 
 
-def slope_rows(mask, x, grad, own, far, inv_own, inv_far, expand, contract):
-    cells = cells_at_once(x.shape[0], 2)
+def slope_rows(mask, first, x, grad, own, far, inv_own, inv_far, expand, contract):
+    count = far.shape[0]
+    cells = cells_at_once(math.gcd(count, first or count), 2)
     points, chan = x.shape[1:]
     hid = expand.shape[1]
-    work = 10 * x.shape[0] * points * expand.size
-    rows = [x, grad, own, far]
+    out = jax.ShapeDtypeStruct((count, points, chan), jnp.bfloat16)
+    work = 10 * count * points * expand.size
     whole = [inv_own, inv_far, inv_own.T, inv_far.T, expand, expand.T, contract.T]
     sums = jax.ShapeDtypeStruct((2, chan, hid), jnp.float32)
     return pl.pallas_call(
-        functools.partial(slope_kernel, cells),
-        grid=(x.shape[0] // cells,),
-        out_shape=[jax.ShapeDtypeStruct(a.shape, jnp.bfloat16) for a in (x, own, far)] + [sums],
+        functools.partial(slope_kernel, cells, first),
+        grid=(count // cells,),
+        out_shape=[out] + [jax.ShapeDtypeStruct(a.shape, jnp.bfloat16) for a in (own, far)] + [sums],
         in_specs=[pl.BlockSpec(memory_space=pltpu.SMEM)]
-        + [row_spec(cells, a) for a in rows]
+        + [row_spec(cells, a, first) for a in (x, grad)]
+        + [row_spec(cells, a) for a in (own, far)]
         + [whole_spec(a) for a in whole],
-        out_specs=[row_spec(cells, a) for a in (x, own, far)] + [whole_spec(sums)],
+        out_specs=[row_spec(cells, a) for a in (out, own, far)] + [whole_spec(sums)],
         scratch_shapes=[
             pltpu.VMEM((cells * points, chan), jnp.bfloat16),
             pltpu.VMEM((cells * points, chan), jnp.bfloat16),
@@ -434,9 +444,11 @@
             pltpu.VMEM((cells * points, hid), jnp.bfloat16),
         ],
         compiler_params=pltpu.CompilerParams(vmem_limit_bytes=VMEM_BYTES),
-        cost_estimate=pl.CostEstimate(flops=4 * work, bytes_accessed=12 * x.size, transcendentals=0),
+        cost_estimate=pl.CostEstimate(
+            flops=2 * work, bytes_accessed=12 * count * points * chan, transcendentals=0
+        ),
         name="slope_rows",
-    )(mask, *rows, *whole)
+    )(mask, x, grad, own, far, *whole)
 
 
 def swap(block, axis, mask=1):
@@ -493,49 +505,81 @@
             "jnc,nk->jkc", x, table, preferred_element_type=jnp.float32
         ).astype(jnp.bfloat16)
 
-    saved_far = swap(longitude(saved, forward_far), "sp")
+    half = slot_count // 2
+    parts = ((0, half), (half, slot_count))
+
+    def exchange(pieces):
+        return [swap(piece, "sp") for piece in pieces]
+
+    def after(values, *before):
+        return lax.optimization_barrier((values,) + before)[0]
+
+    saved_send = longitude(saved, forward_far)
+    saved_far = swap(saved_send, "sp")
     saved_own = longitude(saved, forward_own)
-    fresh_send = longitude(fresh, forward_far)
-    fresh_own = longitude(fresh, forward_own)
+    fresh_later = after(fresh, saved_own)
+    fresh_send = longitude(fresh_later, forward_far)
+    fresh_send = [fresh_send[low:high] for low, high in parts]
+    fresh_far = [swap(after(fresh_send[0], saved_send), "sp")]
+    fresh_own = longitude(fresh_later, forward_own)
     analysis, synthesis = legendre_tables(
         jnp.concatenate([own_cycles, far_cycles]), own_orders, NLAT
     )
 
-    def to_degrees(own, far, table):
-        both = jnp.concatenate([own, far], axis=0)
+    def to_degrees(pieces, table):
+        both = jnp.concatenate(pieces, axis=0)
         both = both.reshape(2 * slot_count, slot_count, 2, chan_count)
         return jnp.einsum("tlj,jtrc->trlc", table, both, preferred_element_type=jnp.float32)
 
-    def to_rows(spectra, table):
+    def to_rows(spectra, table, low, high):
         rows = jnp.einsum(
-            "tlj,trlc->jtrc", table, spectra, preferred_element_type=jnp.float32
+            "tlj,trlc->jtrc", table[:, :, low:high], spectra, preferred_element_type=jnp.float32
         ).astype(jnp.bfloat16)
-        rows = rows.reshape(2 * slot_count, 2 * slot_count, chan_count)
-        return rows[:slot_count], rows[slot_count:]
+        return rows.reshape(high - low, 2 * slot_count, chan_count)
+
+    def own_rows(spectra, table):
+        return [to_rows(spectra, table, low, high) for low, high in parts]
+
+    def far_rows(spectra, table):
+        return [
+            to_rows(spectra, table, slot_count + low, slot_count + high) for low, high in parts
+        ]
 
     def filtered(spectra):
         real_part = filt[0] * spectra[:, 0] - filt[1] * spectra[:, 1]
         imag_part = filt[0] * spectra[:, 1] + filt[1] * spectra[:, 0]
         return jnp.stack([real_part, imag_part], axis=1).astype(jnp.bfloat16)
 
-    spectra = to_degrees(saved_own, saved_far, analysis)
-    own_values, far_values = to_rows(filtered(spectra), synthesis)
-    came_values = swap(far_values, "sp")
-    fresh_far = swap(fresh_send, "sp")
-    fresh_filtered = filtered(to_degrees(fresh_own, fresh_far, analysis))
-    fresh_own_values, fresh_far_values = to_rows(fresh_filtered, synthesis)
-    fresh_came = swap(fresh_far_values, "sp")
-
-    grad_mixed, grad_own, grad_send, sums = slope_rows(
-        cycle_mask, saved, output_grad[0, 0], own_values, came_values, inverse_own, inverse_far,
-        expand, contract,
-    )
-    grad_far = swap(grad_send, "sp")
-    block = value_rows(
-        cycle_mask, fresh, fresh_own_values, fresh_came, inverse_own, inverse_far, expand, contract
-    )
-    next_input = from_behind(block[None, None], "pipe", 1)
-    grad_filtered = to_degrees(grad_own, grad_far, synthesis)
+    spectra = to_degrees([saved_own, saved_far], analysis)
+    saved_filtered = filtered(spectra)
+    send_values = far_rows(saved_filtered, synthesis)
+    send_values[1] = after(send_values[1], send_values[0])
+    came_values = exchange(send_values)
+    fresh_far.append(swap(after(fresh_send[1], send_values), "sp"))
+    own_values = own_rows(after(saved_filtered, send_values), synthesis)
+
+    slopes = []
+    for (low, _), own, came in zip(parts, own_values, came_values):
+        slopes.append(
+            slope_rows(
+                cycle_mask, low, saved, output_grad[0, 0], after(own, slopes), came, inverse_own,
+                inverse_far, expand, contract,
+            )
+        )
+    grad_mixed, grad_own, grad_send, sums = zip(*slopes)
+    grad_far = exchange(grad_send)
+
+    fresh_far = after(fresh_far, grad_send)
+    fresh_filtered = filtered(to_degrees([fresh_own] + fresh_far, analysis))
+    fresh_send_values = far_rows(fresh_filtered, synthesis)
+    fresh_came = exchange(fresh_send_values)
+    fresh_own_values = own_rows(fresh_filtered, synthesis)
+    sums = scatter_sum(sums[0] + sums[1], "dp")
+    scattered = sums
+    sums = sums + swap(sums.astype(jnp.bfloat16), "sp").astype(jnp.float32)
+
+    grad_far = after(list(grad_far), fresh_send_values)
+    grad_filtered = to_degrees(list(grad_own) + grad_far, synthesis)
     filter_real = jnp.sum(
         grad_filtered[:, 0] * spectra[:, 0] + grad_filtered[:, 1] * spectra[:, 1], axis=0
     )
@@ -549,19 +593,44 @@
         ],
         axis=1,
     ).astype(jnp.bfloat16)
-    own_coeffs, far_coeffs = to_rows(grad_spectra, analysis)
-    came_coeffs = swap(far_coeffs, "sp")
-    filter_grad = pair_sum(pair_sum(jnp.stack([filter_real, filter_imag]), "sp"), "dp")
-    sums = sums + swap(sums.astype(jnp.bfloat16), "sp").astype(jnp.float32)
-    sums = scatter_sum(sums, "dp")
-    grad_tokens = jnp.einsum(
-        "jkc,nk->jnc", own_coeffs, forward_own, preferred_element_type=jnp.float32
-    ) + jnp.einsum("jkc,nk->jnc", came_coeffs, forward_far, preferred_element_type=jnp.float32)
-    input_grad = (
-        (grad_mixed.astype(jnp.float32) + grad_tokens) * cycle_mask[:, None, None]
-    ).astype(jnp.bfloat16)
-    sent_back = from_behind(input_grad[None, None], "pipe", -1)
-    return (next_input, sent_back, sums[0][None], sums[1].T[None], filter_grad[None])
+    send_coeffs = far_rows(after(grad_spectra, scattered), analysis)
+    send_coeffs[1] = after(send_coeffs[1], send_coeffs[0])
+    came_coeffs = exchange(send_coeffs)
+    fresh_came = after(fresh_came, send_coeffs)
+    own_coeffs = own_rows(after(grad_spectra, send_coeffs), analysis)
+    filter_grad = pair_sum(jnp.stack([filter_real, filter_imag]), "dp")
+    fresh_came[1] = after(fresh_came[1], filter_grad, sums)
+    filter_grad = pair_sum(filter_grad, "sp")
+
+    def joined(pieces):
+        whole = jnp.zeros((1, 1) + fresh.shape, jnp.bfloat16)
+        for (low, _), piece in zip(parts, pieces):
+            whole = lax.dynamic_update_slice(whole, piece[None, None], (0, 0, low, 0, 0))
+        return whole
+
+    next_pieces, back_pieces = [], []
+    for at, (low, high) in enumerate(parts):
+        block = value_rows(
+            cycle_mask, low, fresh, after(fresh_own_values[at], back_pieces), fresh_came[at],
+            inverse_own, inverse_far, expand, contract,
+        )
+        next_pieces.append(block)
+        grad_tokens = jnp.einsum(
+            "jkc,nk->jnc", own_coeffs[at], forward_own, preferred_element_type=jnp.float32
+        ) + jnp.einsum(
+            "jkc,nk->jnc", came_coeffs[at], forward_far, preferred_element_type=jnp.float32
+        )
+        piece = (grad_mixed[at].astype(jnp.float32) + grad_tokens) * cycle_mask[low:high, None, None]
+        back_pieces.append(piece.astype(jnp.bfloat16))
+    next_pieces = [from_behind(piece, "pipe", 1) for piece in next_pieces]
+    back_pieces = [from_behind(piece, "pipe", -1) for piece in back_pieces]
+    return (
+        joined(next_pieces),
+        joined(back_pieces),
+        sums[0][None],
+        sums[1].T[None],
+        filter_grad[None],
+    )
 
 
 def solution(mesh):

time: 373 us -> 321 us (0.86)
  waiting for transfers between devices: 144 us -> 87.1 us
  local copies, waits for them, and re-layouts: 37.8 us -> 25.5 us
  other arithmetic: 16.5 us -> 23.4 us
  matrix products: 35.9 us -> 40.7 us
  Pallas kernels: 102 us -> 106 us
    ppermute x12 -> x17, waiting for transfers between devices: 139 us -> 74.4 us  [swap(): lax.ppermute(block, axis, [(i, i ^ mask) for i in range(lax.axis_size(axi...]
    slice x8 -> x2, local copies, waits for them, and re-layouts: 20.5 us -> 1.46 us  [the longest x1 1.39 us: paired_on_device(): fresh_send = [fresh_send[low:high] for low, high in parts]]
    convert_element_type x0 -> x8, local copies, waits for them, and re-layouts: none -> 11.5 us  [to_rows(): rows = jnp.einsum('tlj,trlc->jtrc', table[:, :, low:high], spectra, prefe...]
    unnamed x42 -> x36, local copies, waits for them, and re-layouts: 15 us -> 6.02 us
    dot_general x5 -> x16, matrix products: 17.7 us -> 26.1 us  [the longest x12 17 us: to_rows(): jnp.einsum('tlj,trlc->jtrc', table[:, :, low:high], spectra, preferred_el...]
    dynamic_update_slice x0 -> x2, other arithmetic: none -> 7.88 us  [joined(): lax.dynamic_update_slice(whole, piece[None, None], (0, 0, low, 0, 0))]
    ppermute x2 -> x4, waiting for transfers between devices: 4.8 us -> 12.6 us  [from_behind(): return lax.ppermute(block, axis, route)]
    reduce_sum x1, other arithmetic: 6.57 us -> 1.96 us  [paired_on_device(): jnp.sum(grad_filtered[:, 0] * spectra[:, 0] + grad_filtered[:, 1] * spect...]
  transfers between devices with their start and end apart: 14 -> 21, of which waited for: 10 -> 10; matrix products, arithmetic and copies ran while one was open for 12% -> 24% of each run, Pallas kernels for 28% -> 34%
where the time goes in v2:
time: 321 us; the launch traced here: 315 us
  Pallas kernels  106 us (33%)
  waiting for transfers between devices  87.1 us (27%)
  matrix products  40.7 us (13%)
  starting transfers between devices  31.2 us (10%)
  local copies, waits for them, and re-layouts  25.5 us (8%)
  other arithmetic  23.4 us (7%)
    ppermute x17, waiting for transfers between devices, swap(): lax.ppermute(block, axis, [(i, i ^ mask) for i in range(lax.axis_size(axi...  74.4 us
    pallas_call x2, Pallas kernels, slope_rows(): pl.pallas_call(functools.partial(slope_kernel, cells, first), grid=(count...  63.6 us
    pallas_call x2, Pallas kernels, value_rows(): pl.pallas_call(functools.partial(value_kernel, cells, first), grid=(count...  38.4 us
    dot_general x12, matrix products, to_rows(): jnp.einsum('tlj,trlc->jtrc', table[:, :, low:high], spectra, preferred_el...  17 us
    ppermute x17, starting transfers between devices, swap(): lax.ppermute(block, axis, [(i, i ^ mask) for i in range(lax.axis_size(axi...  15.6 us
    ppermute x4, starting transfers between devices, from_behind(): return lax.ppermute(block, axis, route)  15.6 us
    ppermute x4, waiting for transfers between devices, from_behind(): return lax.ppermute(block, axis, route)  12.6 us
    convert_element_type x8, local copies, waits for them, and re-layouts, to_rows(): rows = jnp.einsum('tlj,trlc->jtrc', table[:, :, low:high], spectra, prefe...  11.5 us
  transfers between devices with their start and end apart: 21, of which 10 were waited for; matrix products, arithmetic and copies ran while one was open for 24% of the time, Pallas kernels for 34%

profile of v2, /device:TPU:1, one launch (start us, length us, event | category | flops | bytes accessed | tf_op | source)
XLA Modules:
  0.0 315.2 jit_solution(18011818630512239467)
XLA Ops:
  1.3 3.9 %convert_bitcast_fusion = bf16[60,120,128]{2,1,0:T(8,128)(2,1)} fusion(bf16[240,120,1]{0,1,2:T(8,128)(2,1)S(1)} %reshape.613, bf16[1,1,60,240,128]{4,3,2,1,0:T(8,128)(2,1)} %param.8), kind=kOutput, calls=%fused_computation.66 | convolution fusion | flops 443289600 | bytes 5587200 | tf_op jit(solution)/shard_map/jnc,nk->jkc/dot_general | solution.py:504
  5.3 2.1 collective-permute-start.1
  8.0 2.8 convert_bitcast_fusion.3
  11.9 1.4 fusion.156
  17.5 3.9 %recursion.1 = (bf16[60,120,120]{2,1,0:T(8,128)(2,1)S(1)}, bf16[60,120,120]{2,1,0:T(8,128)(2,1)S(1)}) custom-call(f32[60,120]{1,0:T(8,128)S(1)} %get-tuple-element.115.main_ref, f32[60,120]{1,0:T(8,128)S(1)} %get-tuple-element.114.back_ref, f32[60,120]{1,0:T(8,128)S(1)} %get-tuple-element.116.start_ref, f32[1,120]{1,0:T(1,128)S(1)} %get-tuple-element.100.cos_ref, ...), custom_call_target="tpu_custom_call" | custom-call | flops 10368000 | bytes 20000000 | tf_op jit(solution)/shard_map/recursion/pallas_call | solution.py:310
  21.6 3.9 %convert_bitcast_fusion.2 = bf16[60,120,128]{2,1,0:T(8,128)(2,1)} fusion(bf16[240,120,1]{0,1,2:T(8,128)(2,1)S(1)} %reshape.612, bf16[60,240,128]{2,1,0:T(8,128)(2,1)} %bitcast.259), kind=kOutput, calls=%fused_computation.68 | convolution fusion | flops 443289600 | bytes 5587200 | tf_op jit(solution)/shard_map/jnc,nk->jkc/dot_general | solution.py:504
  25.5 22.0 %collective-permute-done.1 = bf16[60,120,128]{2,1,0:T(8,128)(2,1)} collective-permute-done((bf16[60,120,128]{2,1,0:T(8,128)(2,1)}, bf16[60,120,128]{2,1,0:T(8,128)(2,1)}, u32[]{:S(2)}, u32[]{:S(2)}) %collective-permute-start.1) | collective-permute-done | bytes 1843232 | tf_op jit(solution)/shard_map/ppermute | solution.py:455
  47.5 1.8 pad_maximum_fusion
  49.4 1.1 fusion.10
  50.5 1.0 subtract_convert_fusion.2
  51.5 1.9 copy-done
  53.4 1.7 fusion.109
  55.1 1.7 fusion.103
  57.4 1.2 collective-permute-start.3
  58.7 1.7 copy.57
  63.0 1.7 copy.59
  64.7 1.6 fusion.97
  66.3 1.6 copy.67
  67.9 19.0 %collective-permute-done.3.far_ref = bf16[30,120,128]{2,1,0:T(8,128)(2,1)S(1)} collective-permute-done((bf16[30,120,128]{2,1,0:T(8,128)(2,1)S(1)}, bf16[30,120,128]{2,1,0:T(8,128)(2,1)S(1)}, u32[]{:S(2)}, u32[]{:S(2)}) %collective-permute-start.3) | collective-permute-done | bytes 921632 | tf_op jit(solution)/shard_map/ppermute | solution.py:455
  86.9 1.0 copy-done.14
  87.9 32.0 %slope_rows.2 = (bf16[30,240,128]{2,1,0:T(8,128)(2,1)}, bf16[30,120,128]{2,1,0:T(8,128)(2,1)}, bf16[30,120,128]{2,1,0:T(8,128)(2,1)}, f32[2,128,768]{2,1,0:T(8,128)}) custom-call(f32[60]{0:T(128)} %copy-done.12, bf16[60,240,128]{2,1,0:T(8,128)(2,1)} %bitcast.257, bf16[60,240,128]{2,1,0:T(8,128)(2,1)} %bitcast.294, bf16[30,120,128]{2,1,0:T(8,128)(2,1)} %bitcast.280, ...), custom_call_target="tpu_custom_call" | custom-call | flops 14155776000 | bytes 11059200 | tf_op jit(solution)/shard_map/slope_rows/pallas_call | solution.py:431
  119.8 1.2 collective-permute-start.7
  121.1 31.6 %slope_rows.3 = (bf16[30,240,128]{2,1,0:T(8,128)(2,1)}, bf16[30,120,128]{2,1,0:T(8,128)(2,1)}, bf16[30,120,128]{2,1,0:T(8,128)(2,1)}, f32[2,128,768]{2,1,0:T(8,128)}) custom-call(f32[60]{0:T(128)} %copy-done.12, bf16[60,240,128]{2,1,0:T(8,128)(2,1)} %bitcast.258, bf16[60,240,128]{2,1,0:T(8,128)(2,1)} %bitcast.295, bf16[30,120,128]{2,1,0:T(8,128)(2,1)} %bitcast.278, ...), custom_call_target="tpu_custom_call" | custom-call | flops 14155776000 | bytes 11059200 | tf_op jit(solution)/shard_map/slope_rows/pallas_call | solution.py:431
  152.7 1.6 add.181
  154.7 2.3 collective-permute-start.9
  157.0 2.1 pad_maximum_fusion.2
  159.1 1.1 fusion.13
  160.2 1.0 subtract_convert_fusion.1
  161.2 1.7 fusion.106
  162.9 1.7 fusion.100
  164.5 1.1 collective-permute-done.9
  166.1 1.7 fusion.94
  167.8 2.2 collective-permute-done.10
  172.0 1.3 collective-permute-start.5
  173.3 1.6 copy.78
  175.1 1.7 copy.74
  176.8 1.7 copy.85
  178.6 2.7 pad_maximum_fusion.4
  181.3 1.1 fusion.16
  183.2 2.0 add_reduce_fusion
  185.6 1.6 fusion.85
  187.2 1.6 fusion.82
  188.8 1.3 copy.90
  190.1 1.3 copy.86
  191.4 1.4 collective-permute-start.13
  192.8 1.6 fusion.27
  195.1 1.2 collective-permute-done.5.far_ref
  196.3 19.7 %collective-permute-done.6.far_ref = bf16[30,120,128]{2,1,0:T(8,128)(2,1)} collective-permute-done((bf16[30,120,128]{2,1,0:T(8,128)(2,1)}, bf16[30,120,128]{2,1,0:T(8,128)(2,1)}, u32[]{:S(2)}, u32[]{:S(2)}) %collective-permute-start.6) | collective-permute-done | bytes 921632 | tf_op jit(solution)/shard_map/ppermute | solution.py:455
  217.5 19.0 %value_rows.2 = bf16[30,240,128]{2,1,0:T(8,128)(2,1)} custom-call(f32[60]{0:T(128)} %copy-done.12, bf16[60,240,128]{2,1,0:T(8,128)(2,1)} %bitcast.260, bf16[30,120,128]{2,1,0:T(8,128)(2,1)} %bitcast.276, bf16[30,120,128]{2,1,0:T(8,128)(2,1)} %collective-permute-done.5.far_ref, bf16[240,120]{1,0:T(8,128)(2,1)} %copy.62.inv_own_ref, ...), custom_call_target="tpu_custom_call" | custom-call | flops 5662310400 | bytes 7372800 | tf_op jit(solution)/shard_map/value_rows/pallas_call | solution.py:406
  236.5 7.7 %collective-permute-start.11 = (bf16[30,240,128]{2,1,0:T(8,128)(2,1)}, bf16[30,240,128]{2,1,0:T(8,128)(2,1)}, u32[]{:S(2)}, u32[]{:S(2)}) collective-permute-start(bf16[30,240,128]{2,1,0:T(8,128)(2,1)} %value_rows.2), channel_id=1, source_target_pairs={{0,8},{8,16},{16,24},{1,9},{9,17},{17,25},{2,10},{10,18},{18,26},{... | collective-permute-start | bytes 5529608 | tf_op jit(solution)/shard_map/ppermute | solution.py:22
  244.3 0.9 fusion.113
  245.2 2.4 collective-permute-start.14
  248.5 5.6 %collective-permute-done.14 = f32[2,120,128]{2,1,0:T(8,128)S(1)} collective-permute-done((f32[2,120,128]{2,1,0:T(8,128)S(1)}, f32[2,120,128]{2,1,0:T(8,128)S(1)}, u32[]{:S(2)}, u32[]{:S(2)}) %collective-permute-start.14) | collective-permute-done | bytes 122912 | tf_op jit(solution)/shard_map/ppermute | solution.py:455
  254.2 3.3 %fusion.3 = bf16[30,240,128]{2,1,0:T(8,128)(2,1)} fusion(f32[240,30,128,1]{2,0,3,1:T(8,128)S(1)} %fusion.113, bf16[30,240,128]{2,1,0:T(8,128)(2,1)S(1)} %copy-done.3, bf16[30,120,128]{2,1,0:T(8,128)(2,1)} %collective-permute-done.12, f32[30]{0:T(128)S(1)} %get-tuple-element.102, bf16[240,120]{0,1:T(8,128)(2,1)S(1)} %reshape.596), kind=kOutput, calls=%fused_computation.14 | convolution fusion | flops 225792000 | bytes 8352120 | tf_op jit(solution)/shard_map/jkc,nk->jnc/dot_general | solution.py:620
  257.5 2.3 collective-permute-start.17
  259.9 19.3 %value_rows.3 = bf16[30,240,128]{2,1,0:T(8,128)(2,1)} custom-call(f32[60]{0:T(128)} %copy-done.12, bf16[60,240,128]{2,1,0:T(8,128)(2,1)} %bitcast.261, bf16[30,120,128]{2,1,0:T(8,128)(2,1)} %bitcast.275, bf16[30,120,128]{2,1,0:T(8,128)(2,1)} %collective-permute-done.6.far_ref, bf16[240,120]{1,0:T(8,128)(2,1)} %copy.62.inv_own_ref, ...), custom_call_target="tpu_custom_call" | custom-call | flops 5662310400 | bytes 7372800 | tf_op jit(solution)/shard_map/value_rows/pallas_call | solution.py:406
  279.2 3.2 %collective-permute-start.16 = (bf16[30,240,128]{2,1,0:T(8,128)(2,1)}, bf16[30,240,128]{2,1,0:T(8,128)(2,1)}, u32[]{:S(2)}, u32[]{:S(2)}) collective-permute-start(bf16[30,240,128]{2,1,0:T(8,128)(2,1)} %value_rows.3), channel_id=1, source_target_pairs={{0,8},{8,16},{16,24},{1,9},{9,17},{17,25},{2,10},{10,18},{18,26},{... | collective-permute-start | bytes 5529608 | tf_op jit(solution)/shard_map/ppermute | solution.py:22
  282.4 3.9 %fusion.1 = bf16[30,240,128]{2,1,0:T(8,128)(2,1)} fusion(f32[240,30,128,1]{2,0,3,1:T(8,128)S(1)} %fusion.116, bf16[30,240,128]{2,1,0:T(8,128)(2,1)} %get-tuple-element.58, bf16[30,120,128]{2,1,0:T(8,128)(2,1)} %collective-permute-done.18, f32[30]{0:T(128)S(1)} %get-tuple-element.101, bf16[240,120]{0,1:T(8,128)(2,1)S(1)} %reshape.596), kind=kOutput, calls=%fused_computation.10 | convolution fusion | flops 225792000 | bytes 8352120 | tf_op jit(solution)/shard_map/jkc,nk->jnc/dot_general | solution.py:620
  286.3 2.3 collective-permute-start.19
  290.2 3.5 %collective-permute-done.20 = f32[2,120,128]{2,1,0:T(8,128)S(1)} collective-permute-done((f32[2,120,128]{2,1,0:T(8,128)S(1)}, f32[2,120,128]{2,1,0:T(8,128)S(1)}, u32[]{:S(2)}, u32[]{:S(2)}) %collective-permute-start.20) | collective-permute-done | bytes 122912 | tf_op jit(solution)/shard_map/ppermute | solution.py:455
  294.4 8.6 %collective-permute-done.16 = bf16[30,240,128]{2,1,0:T(8,128)(2,1)} collective-permute-done((bf16[30,240,128]{2,1,0:T(8,128)(2,1)}, bf16[30,240,128]{2,1,0:T(8,128)(2,1)}, u32[]{:S(2)}, u32[]{:S(2)}) %collective-permute-start.16) | collective-permute-done | bytes 1843232 | tf_op jit(solution)/shard_map/ppermute | solution.py:22
  303.0 4.2 %pad_maximum_fusion.6 = bf16[1,1,60,240,128]{4,3,2,1,0:T(8,128)(2,1)} fusion(bf16[1,1,30,240,128]{4,3,2,1,0:T(8,128)(2,1)} %bitcast.75, bf16[1,1,30,240,128]{4,3,2,1,0:T(8,128)(2,1)} %bitcast.61), kind=kLoop, calls=%fused_computation.6 | loop fusion | flops 1843200 | bytes 7372800 | tf_op jit(solution)/shard_map/dynamic_update_slice | solution.py:608
  307.2 4.1 %collective-permute-done.19 = bf16[30,240,128]{2,1,0:T(8,128)(2,1)} collective-permute-done((bf16[30,240,128]{2,1,0:T(8,128)(2,1)}, bf16[30,240,128]{2,1,0:T(8,128)(2,1)}, u32[]{:S(2)}, u32[]{:S(2)}) %collective-permute-start.19) | collective-permute-done | bytes 1843232 | tf_op jit(solution)/shard_map/ppermute | solution.py:22
  311.3 3.7 %pad_maximum_fusion.7 = bf16[1,1,60,240,128]{4,3,2,1,0:T(8,128)(2,1)} fusion(bf16[1,1,30,240,128]{4,3,2,1,0:T(8,128)(2,1)} %bitcast.85, bf16[1,1,30,240,128]{4,3,2,1,0:T(8,128)(2,1)S(1)} %bitcast.268), kind=kLoop, calls=%fused_computation.7 | loop fusion | flops 1843200 | bytes 7372800 | tf_op jit(solution)/shard_map/dynamic_update_slice | solution.py:608
  (114 shorter events, 19.5 us)
Async XLA Ops:
  5.3 42.3 %collective-permute-start.1 = (bf16[60,120,128]{2,1,0:T(8,128)(2,1)}, bf16[60,120,128]{2,1,0:T(8,128)(2,1)}, u32[]{:S(2)}, u32[]{:S(2)}) collective-permute-start(bf16[60,120,128]{2,1,0:T(8,128)(2,1)} %convert_bitcast_fusion), channel_id=1, source_target_pairs={{0,4},{4,0},{1,5},{5,1},{2,6},{6,2},{3,7},{7,3},{8,12},{12,8},{9,1... | collective-permute-start | bytes 5529608 | tf_op jit(solution)/shard_map/ppermute | solution.py:455
  8.0 3.2 %copy-start.1 = (bf16[1,1,60,240,128]{4,3,2,1,0:T(8,128)(2,1)S(1)}, bf16[1,1,60,240,128]{4,3,2,1,0:T(8,128)(2,1)}, u32[]{:S(2)}) copy-start(bf16[1,1,60,240,128]{4,3,2,1,0:T(8,128)(2,1)} %param.7) | copy-start | bytes 11059204
  11.2 2.1 copy-start.13
  11.8 3.5 %copy-start.10 = (bf16[1,768,128]{2,1,0:T(8,128)(2,1)S(1)}, bf16[1,768,128]{2,1,0:T(8,128)(2,1)}, u32[]{:S(2)}) copy-start(bf16[1,768,128]{2,1,0:T(8,128)(2,1)} %param.11) | copy-start | bytes 589828
  11.9 4.3 %copy-start.9 = (bf16[1,128,768]{2,1,0:T(8,128)(2,1)S(1)}, bf16[1,128,768]{2,1,0:T(8,128)(2,1)}, u32[]{:S(2)}) copy-start(bf16[1,128,768]{2,1,0:T(8,128)(2,1)} %param.10) | copy-start | bytes 589828
  11.9 9.7 %copy-start.11 = (f32[1,2,120,128]{3,2,1,0:T(8,128)S(1)}, f32[1,2,120,128]{3,2,1,0:T(8,128)}, u32[]{:S(2)}) copy-start(f32[1,2,120,128]{3,2,1,0:T(8,128)} %param.12) | copy-start | bytes 368644
  13.3 141.4 %collective-permute-start = (bf16[30,120,128]{2,1,0:T(8,128)(2,1)}, bf16[30,120,128]{2,1,0:T(8,128)(2,1)}, u32[]{:S(2)}, u32[]{:S(2)}) collective-permute-start(bf16[30,120,128]{2,1,0:T(8,128)(2,1)} %get-tuple-element.33), channel_id=1, source_target_pairs={{0,4},{4,0},{1,5},{5,1},{2,6},{6,2},{3,7},{7,3},{8,12},{12,8},{9,1... | collective-permute-start | bytes 2764808 | tf_op jit(solution)/shard_map/ppermute | solution.py:455
  13.7 11.8 %copy-start.7 = (bf16[240,120]{0,1:T(8,128)(2,1)}, bf16[240,120]{0,1:T(8,128)(2,1)S(1)}, u32[]{:S(2)}) copy-start(bf16[240,120]{0,1:T(8,128)(2,1)S(1)} %reshape.601) | copy-start | bytes 172804
  14.6 34.8 %copy-start.8 = (bf16[240,120]{0,1:T(8,128)(2,1)}, bf16[240,120]{0,1:T(8,128)(2,1)S(1)}, u32[]{:S(2)}) copy-start(bf16[240,120]{0,1:T(8,128)(2,1)S(1)} %reshape.602) | copy-start | bytes 172804
  17.0 32.4 %copy-start.12 = (f32[60]{0:T(128)}, f32[60]{0:T(128)S(1)}, u32[]{:S(2)}) copy-start(f32[60]{0:T(128)S(1)} %get-tuple-element.75.mask_ref) | copy-start | bytes 724
  50.5 2.9 copy-start
  57.4 29.5 %collective-permute-start.3 = (bf16[30,120,128]{2,1,0:T(8,128)(2,1)S(1)}, bf16[30,120,128]{2,1,0:T(8,128)(2,1)S(1)}, u32[]{:S(2)}, u32[]{:S(2)}) collective-permute-start(bf16[30,120,128]{2,1,0:T(8,128)(2,1)S(1)} %bitcast.279), channel_id=1, source_target_pairs={{0,4},{4,0},{1,5},{5,1},{2,6},{6,2},{3,7},{7,3},{8,12},{12,8},{9,1... | collective-permute-start | bytes 2764808 | tf_op jit(solution)/shard_map/ppermute | solution.py:455
  60.4 1.2 copy-start.6
  60.4 60.7 %collective-permute-start.4 = (bf16[30,120,128]{2,1,0:T(8,128)(2,1)}, bf16[30,120,128]{2,1,0:T(8,128)(2,1)}, u32[]{:S(2)}, u32[]{:S(2)}) collective-permute-start(bf16[30,120,128]{2,1,0:T(8,128)(2,1)} %bitcast.21), channel_id=1, source_target_pairs={{0,4},{4,0},{1,5},{5,1},{2,6},{6,2},{3,7},{7,3},{8,12},{12,8},{9,1... | collective-permute-start | bytes 2764808 | tf_op jit(solution)/shard_map/ppermute | solution.py:455
  61.6 93.1 %collective-permute-start.2 = (bf16[30,120,128]{2,1,0:T(8,128)(2,1)S(1)}, bf16[30,120,128]{2,1,0:T(8,128)(2,1)S(1)}, u32[]{:S(2)}, u32[]{:S(2)}) collective-permute-start(bf16[30,120,128]{2,1,0:T(8,128)(2,1)S(1)} %copy-done.6), channel_id=1, source_target_pairs={{0,4},{4,0},{1,5},{5,1},{2,6},{6,2},{3,7},{7,3},{8,12},{12,8},{9,1... | collective-permute-start | bytes 2764808 | tf_op jit(solution)/shard_map/ppermute | solution.py:455
  86.9 1.0 copy-start.14
  119.8 58.7 %collective-permute-start.7 = (bf16[30,120,128]{2,1,0:T(8,128)(2,1)}, bf16[30,120,128]{2,1,0:T(8,128)(2,1)}, u32[]{:S(2)}, u32[]{:S(2)}) collective-permute-start(bf16[30,120,128]{2,1,0:T(8,128)(2,1)} %get-tuple-element.39), channel_id=1, source_target_pairs={{0,4},{4,0},{1,5},{5,1},{2,6},{6,2},{3,7},{7,3},{8,12},{12,8},{9,1... | collective-permute-start | bytes 2764808 | tf_op jit(solution)/shard_map/ppermute | solution.py:455
  152.7 4.3 %copy-start.2 = (bf16[60,120,128]{2,1,0:T(8,128)(2,1)S(1)}, bf16[60,120,128]{2,1,0:T(8,128)(2,1)}, u32[]{:S(2)}) copy-start(bf16[60,120,128]{2,1,0:T(8,128)(2,1)} %convert_bitcast_fusion.2) | copy-start | bytes 5529604
  154.3 24.3 %collective-permute-start.8 = (bf16[30,120,128]{2,1,0:T(8,128)(2,1)}, bf16[30,120,128]{2,1,0:T(8,128)(2,1)S(1)}, u32[]{:S(2)}, u32[]{:S(2)}) collective-permute-start(bf16[30,120,128]{2,1,0:T(8,128)(2,1)} %get-tuple-element.44), channel_id=1, source_target_pairs={{0,4},{4,0},{1,5},{5,1},{2,6},{6,2},{3,7},{7,3},{8,12},{12,8},{9,1... | collective-permute-start | bytes 2764808 | tf_op jit(solution)/shard_map/ppermute | solution.py:455
  154.7 10.9 %collective-permute-start.9 = (bf16[2,128,384]{2,1,0:T(8,128)(2,1)S(1)}, bf16[2,128,384]{2,1,0:T(8,128)(2,1)S(1)}, u32[]{:S(2)}, u32[]{:S(2)}) collective-permute-start(bf16[2,128,384]{2,1,0:T(8,128)(2,1)S(1)} %select_convert_fusion), channel_id=1, source_target_pairs={{0,2},{1,3},{2,0},{3,1},{4,6},{5,7},{6,4},{7,5},{8,10},{9,11},{10,... | collective-permute-start | bytes 589832 | tf_op jit(solution)/shard_map/ppermute | solution.py:455
  165.8 4.2 %collective-permute-start.10 = (bf16[2,128,192]{2,1,0:T(8,128)(2,1)S(1)}, bf16[2,128,192]{2,1,0:T(8,128)(2,1)S(1)}, u32[]{:S(2)}, u32[]{:S(2)}) collective-permute-start(bf16[2,128,192]{2,1,0:T(8,128)(2,1)S(1)} %select_convert_fusion.1), channel_id=1, source_target_pairs={{0,1},{1,0},{2,3},{3,2},{4,5},{5,4},{6,7},{7,6},{8,9},{9,8},{10,11... | collective-permute-start | bytes 294920 | tf_op jit(solution)/shard_map/ppermute | solution.py:455
  170.1 8.4 %collective-permute-start.15 = (bf16[2,128,192]{2,1,0:T(8,128)(2,1)S(1)}, bf16[2,128,192]{2,1,0:T(8,128)(2,1)S(1)}, u32[]{:S(2)}, u32[]{:S(2)}) collective-permute-start(bf16[2,128,192]{2,1,0:T(8,128)(2,1)S(1)} %get-tuple-element.71), channel_id=1, source_target_pairs={{0,4},{4,0},{1,5},{5,1},{2,6},{6,2},{3,7},{7,3},{8,12},{12,8},{9,1... | collective-permute-start | bytes 294920 | tf_op jit(solution)/shard_map/ppermute | solution.py:455
  171.2 7.4 %copy-start.4 = (bf16[30,120,128]{2,1,0:T(8,128)(2,1)S(1)}, bf16[30,120,128]{2,1,0:T(8,128)(2,1)}, u32[]{:S(2)}) copy-start(bf16[30,120,128]{2,1,0:T(8,128)(2,1)} %get-tuple-element.41) | copy-start | bytes 2764804
  171.2 7.4 %copy-start.5 = (bf16[30,120,128]{2,1,0:T(8,128)(2,1)S(1)}, bf16[30,120,128]{2,1,0:T(8,128)(2,1)}, u32[]{:S(2)}) copy-start(bf16[30,120,128]{2,1,0:T(8,128)(2,1)} %get-tuple-element.47) | copy-start | bytes 2764804
  172.0 24.3 %collective-permute-start.5 = (bf16[30,120,128]{2,1,0:T(8,128)(2,1)S(1)}, bf16[30,120,128]{2,1,0:T(8,128)(2,1)}, u32[]{:S(2)}, u32[]{:S(2)}) collective-permute-start(bf16[30,120,128]{2,1,0:T(8,128)(2,1)S(1)} %bitcast.277), channel_id=1, source_target_pairs={{0,4},{4,0},{1,5},{5,1},{2,6},{6,2},{3,7},{7,3},{8,12},{12,8},{9,1... | collective-permute-start | bytes 2764808 | tf_op jit(solution)/shard_map/ppermute | solution.py:455
  174.9 41.1 %collective-permute-start.6 = (bf16[30,120,128]{2,1,0:T(8,128)(2,1)}, bf16[30,120,128]{2,1,0:T(8,128)(2,1)}, u32[]{:S(2)}, u32[]{:S(2)}) collective-permute-start(bf16[30,120,128]{2,1,0:T(8,128)(2,1)} %bitcast.49), channel_id=1, source_target_pairs={{0,4},{4,0},{1,5},{5,1},{2,6},{6,2},{3,7},{7,3},{8,12},{12,8},{9,1... | collective-permute-start | bytes 2764808 | tf_op jit(solution)/shard_map/ppermute | solution.py:455
  178.6 3.8 %slice-start = ((s8[7372800]{0:T(1024)(128)(4,1)}), s8[4194304]{0:T(1024)(128)(4,1)S(1)}, s32[]{:S(2)}) async-start(s8[7372800]{0:T(1024)(128)(4,1)} %bitcast.255), calls=%async_computation | async-start | bytes 8388608
  181.3 1.9 slice-start.1
  191.4 53.8 %collective-permute-start.13 = (f32[2,120,128]{2,1,0:T(8,128)S(1)}, f32[2,120,128]{2,1,0:T(8,128)S(1)}, u32[]{:S(2)}, u32[]{:S(2)}) collective-permute-start(f32[2,120,128]{2,1,0:T(8,128)S(1)} %pad_maximum_fusion.8), channel_id=1, source_target_pairs={{0,1},{1,0},{2,3},{3,2},{4,5},{5,4},{6,7},{7,6},{8,9},{9,8},{10,11... | collective-permute-start | bytes 368648 | tf_op jit(solution)/shard_map/ppermute | solution.py:455
  216.1 38.1 %collective-permute-start.12 = (bf16[30,120,128]{2,1,0:T(8,128)(2,1)}, bf16[30,120,128]{2,1,0:T(8,128)(2,1)}, u32[]{:S(2)}, u32[]{:S(2)}) collective-permute-start(bf16[30,120,128]{2,1,0:T(8,128)(2,1)} %copy.86), channel_id=1, source_target_pairs={{0,4},{4,0},{1,5},{5,1},{2,6},{6,2},{3,7},{7,3},{8,12},{12,8},{9,1... | collective-permute-start | bytes 2764808 | tf_op jit(solution)/shard_map/ppermute | solution.py:455
  216.9 65.6 %collective-permute-start.18 = (bf16[30,120,128]{2,1,0:T(8,128)(2,1)}, bf16[30,120,128]{2,1,0:T(8,128)(2,1)}, u32[]{:S(2)}, u32[]{:S(2)}) collective-permute-start(bf16[30,120,128]{2,1,0:T(8,128)(2,1)} %copy.90), channel_id=1, source_target_pairs={{0,4},{4,0},{1,5},{5,1},{2,6},{6,2},{3,7},{7,3},{8,12},{12,8},{9,1... | collective-permute-start | bytes 2764808 | tf_op jit(solution)/shard_map/ppermute | solution.py:455
  236.5 57.9 %collective-permute-start.11 = (bf16[30,240,128]{2,1,0:T(8,128)(2,1)}, bf16[30,240,128]{2,1,0:T(8,128)(2,1)}, u32[]{:S(2)}, u32[]{:S(2)}) collective-permute-start(bf16[30,240,128]{2,1,0:T(8,128)(2,1)} %value_rows.2), channel_id=1, source_target_pairs={{0,8},{8,16},{16,24},{1,9},{9,17},{17,25},{2,10},{10,18},{18,26},{... | collective-permute-start | bytes 5529608 | tf_op jit(solution)/shard_map/ppermute | solution.py:22
  245.2 9.0 %copy-start.3 = (bf16[30,240,128]{2,1,0:T(8,128)(2,1)S(1)}, bf16[30,240,128]{2,1,0:T(8,128)(2,1)}, u32[]{:S(2)}) copy-start(bf16[30,240,128]{2,1,0:T(8,128)(2,1)} %get-tuple-element.40) | copy-start | bytes 5529604
  245.2 8.9 %collective-permute-start.14 = (f32[2,120,128]{2,1,0:T(8,128)S(1)}, f32[2,120,128]{2,1,0:T(8,128)S(1)}, u32[]{:S(2)}, u32[]{:S(2)}) collective-permute-start(f32[2,120,128]{2,1,0:T(8,128)S(1)} %fusion.154), channel_id=1, source_target_pairs={{0,2},{1,3},{2,0},{3,1},{4,6},{5,7},{6,4},{7,5},{8,10},{9,11},{10,... | collective-permute-start | bytes 368648 | tf_op jit(solution)/shard_map/ppermute | solution.py:455
  257.5 49.7 %collective-permute-start.17 = (bf16[30,240,128]{2,1,0:T(8,128)(2,1)}, bf16[30,240,128]{2,1,0:T(8,128)(2,1)S(1)}, u32[]{:S(2)}, u32[]{:S(2)}) collective-permute-start(bf16[30,240,128]{2,1,0:T(8,128)(2,1)} %fusion.3), channel_id=1, source_target_pairs={{8,0},{16,8},{24,16},{9,1},{17,9},{25,17},{10,2},{18,10},{26,18},{... | collective-permute-start | bytes 5529608 | tf_op jit(solution)/shard_map/ppermute | solution.py:22
  279.2 23.8 %collective-permute-start.16 = (bf16[30,240,128]{2,1,0:T(8,128)(2,1)}, bf16[30,240,128]{2,1,0:T(8,128)(2,1)}, u32[]{:S(2)}, u32[]{:S(2)}) collective-permute-start(bf16[30,240,128]{2,1,0:T(8,128)(2,1)} %value_rows.3), channel_id=1, source_target_pairs={{0,8},{8,16},{16,24},{1,9},{9,17},{17,25},{2,10},{10,18},{18,26},{... | collective-permute-start | bytes 5529608 | tf_op jit(solution)/shard_map/ppermute | solution.py:22
  286.3 24.9 %collective-permute-start.19 = (bf16[30,240,128]{2,1,0:T(8,128)(2,1)}, bf16[30,240,128]{2,1,0:T(8,128)(2,1)}, u32[]{:S(2)}, u32[]{:S(2)}) collective-permute-start(bf16[30,240,128]{2,1,0:T(8,128)(2,1)} %fusion.1), channel_id=1, source_target_pairs={{8,0},{16,8},{24,16},{9,1},{17,9},{25,17},{10,2},{18,10},{26,18},{... | collective-permute-start | bytes 5529608 | tf_op jit(solution)/shard_map/ppermute | solution.py:22
  288.7 5.1 %collective-permute-start.20 = (f32[2,120,128]{2,1,0:T(8,128)S(1)}, f32[2,120,128]{2,1,0:T(8,128)S(1)}, u32[]{:S(2)}, u32[]{:S(2)}) collective-permute-start(f32[2,120,128]{2,1,0:T(8,128)S(1)} %fusion.172), channel_id=1, source_target_pairs={{0,4},{4,0},{1,5},{5,1},{2,6},{6,2},{3,7},{7,3},{8,12},{12,8},{9,1... | collective-permute-start | bytes 368648 | tf_op jit(solution)/shard_map/ppermute | solution.py:455

commit v3 on v2

--- a/solution.py
+++ b/solution.py
@@ -263,15 +263,23 @@
     cosine = jnp.broadcast_to(cos_ref[...], (order_count, slots))
     previous = jnp.zeros_like(start)
     earlier = jnp.zeros_like(start)
-    for degree in range(cycles):
-        rising = main_ref[:, degree : degree + 1] * (
-            cosine * previous - back_ref[:, degree : degree + 1] * earlier
-        )
-        current = jnp.where(
-            orders == float(degree), start, jnp.where(orders < float(degree), rising, 0.0)
-        )
-        table_ref[:, degree, :] = current
-        previous, earlier = current, previous
+    step = main_ref.shape[2]
+
+    def advance(block, state_pair):
+        previous, earlier = state_pair
+        main, back = main_ref[block], back_ref[block]
+        for at in range(step):
+            degree = block * step + at
+            rising = main[:, at : at + 1] * (cosine * previous - back[:, at : at + 1] * earlier)
+            reached = degree.astype(jnp.float32)
+            current = jnp.where(
+                orders == reached, start, jnp.where(orders < reached, rising, 0.0)
+            )
+            table_ref[:, degree, :] = current
+            previous, earlier = current, previous
+        return previous, earlier
+
+    lax.fori_loop(0, cycles // step, advance, (previous, earlier))
     weight = weight_ref[...]
 
     @pl.loop(0, order_count)
@@ -304,6 +312,11 @@
         jnp.maximum((degree - 1.0) ** 2 - order_value * order_value, 0.0)
         / jnp.maximum(4.0 * (degree - 1.0) ** 2 - 1.0, 1.0)
     )
+    step = math.gcd(cycles, 8)
+    ratio_main, ratio_back = (
+        ratio.reshape(-1, cycles // step, step).transpose(1, 0, 2)
+        for ratio in (ratio_main, ratio_back)
+    )
     weight = cycle_weights(lat_index, cycles)[None, :]
     order_count, slots = starting.shape
     shape = (order_count, cycles, slots)
@@ -408,7 +421,7 @@
         grid=(count // cells,),
         out_shape=out,
         in_specs=[pl.BlockSpec(memory_space=pltpu.SMEM), row_spec(cells, x, first)]
-        + [row_spec(cells, a) for a in (own, far)]
+        + [row_spec(cells, own, first), row_spec(cells, far)]
         + [whole_spec(a) for a in (inv_own, inv_far, expand, contract)],
         out_specs=row_spec(cells, out),
         compiler_params=pltpu.CompilerParams(vmem_limit_bytes=VMEM_BYTES),
@@ -431,12 +444,12 @@
     return pl.pallas_call(
         functools.partial(slope_kernel, cells, first),
         grid=(count // cells,),
-        out_shape=[out] + [jax.ShapeDtypeStruct(a.shape, jnp.bfloat16) for a in (own, far)] + [sums],
+        out_shape=[out] + [jax.ShapeDtypeStruct(a.shape, jnp.bfloat16) for a in (far, far)] + [sums],
         in_specs=[pl.BlockSpec(memory_space=pltpu.SMEM)]
-        + [row_spec(cells, a, first) for a in (x, grad)]
-        + [row_spec(cells, a) for a in (own, far)]
+        + [row_spec(cells, a, first) for a in (x, grad, own)]
+        + [row_spec(cells, far)]
         + [whole_spec(a) for a in whole],
-        out_specs=[row_spec(cells, a) for a in (out, own, far)] + [whole_spec(sums)],
+        out_specs=[row_spec(cells, a) for a in (out, far, far)] + [whole_spec(sums)],
         scratch_shapes=[
             pltpu.VMEM((cells * points, chan), jnp.bfloat16),
             pltpu.VMEM((cells * points, chan), jnp.bfloat16),
@@ -538,12 +551,11 @@
         return rows.reshape(high - low, 2 * slot_count, chan_count)
 
     def own_rows(spectra, table):
-        return [to_rows(spectra, table, low, high) for low, high in parts]
+        return to_rows(spectra, table, 0, slot_count)
 
     def far_rows(spectra, table):
-        return [
-            to_rows(spectra, table, slot_count + low, slot_count + high) for low, high in parts
-        ]
+        rows = to_rows(spectra, table, slot_count, 2 * slot_count)
+        return [rows[low:high] for low, high in parts]
 
     def filtered(spectra):
         real_part = filt[0] * spectra[:, 0] - filt[1] * spectra[:, 1]
@@ -559,10 +571,10 @@
     own_values = own_rows(after(saved_filtered, send_values), synthesis)
 
     slopes = []
-    for (low, _), own, came in zip(parts, own_values, came_values):
+    for (low, _), came in zip(parts, came_values):
         slopes.append(
             slope_rows(
-                cycle_mask, low, saved, output_grad[0, 0], after(own, slopes), came, inverse_own,
+                cycle_mask, low, saved, output_grad[0, 0], after(own_values, slopes), came, inverse_own,
                 inverse_far, expand, contract,
             )
         )
@@ -596,7 +608,7 @@
     send_coeffs = far_rows(after(grad_spectra, scattered), analysis)
     send_coeffs[1] = after(send_coeffs[1], send_coeffs[0])
     came_coeffs = exchange(send_coeffs)
-    fresh_came = after(fresh_came, send_coeffs)
+    fresh_came[0] = after(fresh_came[0], send_coeffs)
     own_coeffs = own_rows(after(grad_spectra, send_coeffs), analysis)
     filter_grad = pair_sum(jnp.stack([filter_real, filter_imag]), "dp")
     fresh_came[1] = after(fresh_came[1], filter_grad, sums)
@@ -608,24 +620,26 @@
             whole = lax.dynamic_update_slice(whole, piece[None, None], (0, 0, low, 0, 0))
         return whole
 
-    next_pieces, back_pieces = [], []
+    blocks, back_pieces = [], []
     for at, (low, high) in enumerate(parts):
-        block = value_rows(
-            cycle_mask, low, fresh, after(fresh_own_values[at], back_pieces), fresh_came[at],
-            inverse_own, inverse_far, expand, contract,
-        )
-        next_pieces.append(block)
+        blocks.append(
+            value_rows(
+                cycle_mask, low, fresh, after(fresh_own_values, back_pieces), fresh_came[at],
+                inverse_own, inverse_far, expand, contract,
+            )
+        )
         grad_tokens = jnp.einsum(
-            "jkc,nk->jnc", own_coeffs[at], forward_own, preferred_element_type=jnp.float32
+            "jkc,nk->jnc", own_coeffs[low:high], forward_own, preferred_element_type=jnp.float32
         ) + jnp.einsum(
-            "jkc,nk->jnc", came_coeffs[at], forward_far, preferred_element_type=jnp.float32
+            "jkc,nk->jnc", after(came_coeffs[at], blocks), forward_far, preferred_element_type=jnp.float32
         )
         piece = (grad_mixed[at].astype(jnp.float32) + grad_tokens) * cycle_mask[low:high, None, None]
         back_pieces.append(piece.astype(jnp.bfloat16))
-    next_pieces = [from_behind(piece, "pipe", 1) for piece in next_pieces]
-    back_pieces = [from_behind(piece, "pipe", -1) for piece in back_pieces]
+    next_input = joined([from_behind(block, "pipe", 1) for block in blocks])
+    first_back = from_behind(back_pieces[0], "pipe", -1)
+    back_pieces = [first_back, from_behind(after(back_pieces[1], first_back), "pipe", -1)]
     return (
-        joined(next_pieces),
+        next_input,
         joined(back_pieces),
         sums[0][None],
         sums[1].T[None],

time: 321 us -> 321 us (level)
  matrix products: 40.7 us -> 29 us
  waiting for transfers between devices: 87.1 us -> 94.2 us
  other arithmetic: 23.4 us -> 28 us
    dot_general x12 -> x6, matrix products: 17 us -> 7.93 us  [to_rows(): jnp.einsum('tlj,trlc->jtrc', table[:, :, low:high], spectra, preferred_el...]
    slice x0 -> x9, local copies, waits for them, and re-layouts: none -> 8.3 us  [the longest x8 7.74 us: far_rows(): return [rows[low:high] for low, high in parts]]
    convert_element_type x8 -> x2, local copies, waits for them, and re-layouts: 11.5 us -> 6.25 us  [to_rows(): rows = jnp.einsum('tlj,trlc->jtrc', table[:, :, low:high], spectra, prefe...]
    ppermute x17, waiting for transfers between devices: 74.4 us -> 79.3 us  [swap(): lax.ppermute(block, axis, [(i, i ^ mask) for i in range(lax.axis_size(axi...]
    dot_general x4, matrix products: 11.3 us -> 8.05 us  [longitude(): jnp.einsum('jnc,nk->jkc', x, table, preferred_element_type=jnp.float32)]
  transfers between devices with their start and end apart: 21 -> 21, of which waited for: 10 -> 9; matrix products, arithmetic and copies ran while one was open for 24% -> 22% of each run, Pallas kernels for 34% -> 34%
where the time goes in v3:
time: 321 us; the launch traced here: 317 us
  Pallas kernels  107 us (33%)
  waiting for transfers between devices  94.2 us (29%)
  starting transfers between devices  30.8 us (10%)
  matrix products  29 us (9%)
  other arithmetic  28 us (9%)
  local copies, waits for them, and re-layouts  26.9 us (8%)
    ppermute x17, waiting for transfers between devices, swap(): lax.ppermute(block, axis, [(i, i ^ mask) for i in range(lax.axis_size(axi...  79.3 us
    pallas_call x2, Pallas kernels, slope_rows(): pl.pallas_call(functools.partial(slope_kernel, cells, first), grid=(count...  63.5 us
    pallas_call x2, Pallas kernels, value_rows(): pl.pallas_call(functools.partial(value_kernel, cells, first), grid=(count...  38.2 us
    ppermute x17, starting transfers between devices, swap(): lax.ppermute(block, axis, [(i, i ^ mask) for i in range(lax.axis_size(axi...  17.2 us
    ppermute x4, waiting for transfers between devices, from_behind(): return lax.ppermute(block, axis, route)  14.9 us
    ppermute x4, starting transfers between devices, from_behind(): return lax.ppermute(block, axis, route)  13.6 us
    dot_general x4, matrix products, longitude(): jnp.einsum('jnc,nk->jkc', x, table, preferred_element_type=jnp.float32)  8.05 us
    dot_general x6, matrix products, to_rows(): jnp.einsum('tlj,trlc->jtrc', table[:, :, low:high], spectra, preferred_el...  7.93 us
  transfers between devices with their start and end apart: 21, of which 9 were waited for; matrix products, arithmetic and copies ran while one was open for 22% of the time, Pallas kernels for 34%

profile of v3, /device:TPU:1, one launch (start us, length us, event | category | flops | bytes accessed | tf_op | source)
XLA Modules:
  0.0 317.0 jit_solution(15499613359740794758)
XLA Ops:
  1.3 3.9 %convert_bitcast_fusion.6 = bf16[60,120,128]{2,1,0:T(8,128)(2,1)} fusion(bf16[240,120,1]{0,1,2:T(8,128)(2,1)S(1)} %reshape.624, bf16[1,1,60,240,128]{4,3,2,1,0:T(8,128)(2,1)} %param.8), kind=kOutput, calls=%fused_computation.56 | convolution fusion | flops 443289600 | bytes 5587200 | tf_op jit(solution)/shard_map/jnc,nk->jkc/dot_general | solution.py:517
  5.3 2.1 collective-permute-start.1
  8.0 2.8 convert_bitcast_fusion.9
  11.9 1.4 fusion.101
  15.2 0.8 copy.101.contract_t_ref
  17.9 5.0 %recursion.1 = (bf16[60,120,120]{2,1,0:T(8,128)(2,1)S(1)}, bf16[60,120,120]{2,1,0:T(8,128)(2,1)S(1)}) custom-call(f32[15,60,8]{2,1,0:T(8,128)S(1)} %get-tuple-element.132.main_ref, f32[15,60,8]{2,1,0:T(8,128)S(1)} %get-tuple-element.131.back_ref, f32[60,120]{1,0:T(8,128)S(1)} %multiply_multiply_fusion.start_ref, f32[1,120]{1,0:T(1,128)S(1)} %get-tuple-element.113.cos_ref, ...), custom_call_target="tpu_custom_call" | custom-call | flops 10368000 | bytes 20000000 | tf_op jit(solution)/shard_map/recursion/pallas_call | solution.py:323
  23.0 24.6 %collective-permute-done.1 = bf16[60,120,128]{2,1,0:T(8,128)(2,1)} collective-permute-done((bf16[60,120,128]{2,1,0:T(8,128)(2,1)}, bf16[60,120,128]{2,1,0:T(8,128)(2,1)}, u32[]{:S(2)}, u32[]{:S(2)}) %collective-permute-start.1) | collective-permute-done | bytes 1843232 | tf_op jit(solution)/shard_map/ppermute | solution.py:468
  47.5 1.8 pad_maximum_fusion
  49.4 1.1 fusion.10
  50.5 1.0 subtract_convert_fusion.2
  51.5 2.1 copy-done
  53.5 1.7 convert_bitcast_fusion.5
  56.6 1.3 collective-permute-start.3
  58.5 1.7 copy.93
  61.2 0.8 convert_bitcast_fusion.4
  62.1 3.1 copy.95
  66.0 20.9 %collective-permute-done.3.far_ref = bf16[30,120,128]{2,1,0:T(8,128)(2,1)S(1)} collective-permute-done((bf16[30,120,128]{2,1,0:T(8,128)(2,1)S(1)}, bf16[30,120,128]{2,1,0:T(8,128)(2,1)S(1)}, u32[]{:S(2)}, u32[]{:S(2)}) %collective-permute-start.3) | collective-permute-done | bytes 921632 | tf_op jit(solution)/shard_map/ppermute | solution.py:468
  86.9 0.9 copy-done.21
  87.9 31.9 %slope_rows.2 = (bf16[30,240,128]{2,1,0:T(8,128)(2,1)}, bf16[30,120,128]{2,1,0:T(8,128)(2,1)}, bf16[30,120,128]{2,1,0:T(8,128)(2,1)}, f32[2,128,768]{2,1,0:T(8,128)}) custom-call(f32[60]{0:T(128)} %copy-done.18, bf16[60,240,128]{2,1,0:T(8,128)(2,1)} %bitcast.188, bf16[60,240,128]{2,1,0:T(8,128)(2,1)} %bitcast.225, bf16[60,120,128]{2,1,0:T(8,128)(2,1)} %bitcast.202, ...), custom_call_target="tpu_custom_call" | custom-call | flops 14155776000 | bytes 11059200 | tf_op jit(solution)/shard_map/slope_rows/pallas_call | solution.py:444
  119.8 1.2 collective-permute-start.6
  121.0 31.6 %slope_rows.3 = (bf16[30,240,128]{2,1,0:T(8,128)(2,1)}, bf16[30,120,128]{2,1,0:T(8,128)(2,1)}, bf16[30,120,128]{2,1,0:T(8,128)(2,1)}, f32[2,128,768]{2,1,0:T(8,128)}) custom-call(f32[60]{0:T(128)} %copy-done.18, bf16[60,240,128]{2,1,0:T(8,128)(2,1)} %bitcast.189, bf16[60,240,128]{2,1,0:T(8,128)(2,1)} %bitcast.226, bf16[60,120,128]{2,1,0:T(8,128)(2,1)} %bitcast.203, ...), custom_call_target="tpu_custom_call" | custom-call | flops 14155776000 | bytes 11059200 | tf_op jit(solution)/shard_map/slope_rows/pallas_call | solution.py:444
  152.6 1.5 add.187
  154.5 2.3 collective-permute-start.8
  156.8 2.4 pad_maximum_fusion.2
  159.2 1.1 fusion.13
  160.3 1.0 subtract_convert_fusion.1
  161.3 1.7 convert_bitcast_fusion.2
  163.0 1.0 convert_bitcast_fusion.3
  164.0 1.3 collective-permute-done.8
  166.2 3.1 copy.108
  169.3 1.6 copy.111
  171.7 1.3 collective-permute-start.5
  174.0 1.2 collective-permute-start.15
  175.2 2.5 pad_maximum_fusion.4
  177.8 1.1 fusion.16
  179.6 2.1 add_reduce_fusion
  183.2 1.7 convert_bitcast_fusion.1
  185.5 1.3 copy.118
  186.8 1.4 collective-permute-start.11
  188.2 0.9 convert_bitcast_fusion
  189.6 4.6 %collective-permute-done.5.far_ref = bf16[30,120,128]{2,1,0:T(8,128)(2,1)S(1)} collective-permute-done((bf16[30,120,128]{2,1,0:T(8,128)(2,1)S(1)}, bf16[30,120,128]{2,1,0:T(8,128)(2,1)S(1)}, u32[]{:S(2)}, u32[]{:S(2)}) %collective-permute-start.5) | collective-permute-done | bytes 921632 | tf_op jit(solution)/shard_map/ppermute | solution.py:468
  194.2 0.9 fusion.54
  195.2 19.0 %value_rows.2 = bf16[30,240,128]{2,1,0:T(8,128)(2,1)} custom-call(f32[60]{0:T(128)} %copy-done.18, bf16[60,240,128]{2,1,0:T(8,128)(2,1)} %bitcast.190, bf16[60,120,128]{2,1,0:T(8,128)(2,1)} %bitcast.200, bf16[30,120,128]{2,1,0:T(8,128)(2,1)} %copy-done.20, bf16[240,120]{1,0:T(8,128)(2,1)} %copy.98.inv_own_ref, bf16[240,120]{1,0:T(8,128)(2,1)} %copy.99.inv_far_ref, ...), custom_call_target="tpu_custom_call" | custom-call | flops 5662310400 | bytes 7372800 | tf_op jit(solution)/shard_map/value_rows/pallas_call | solution.py:419
  214.2 22.4 %collective-permute-done.11 = bf16[30,120,128]{2,1,0:T(8,128)(2,1)} collective-permute-done((bf16[30,120,128]{2,1,0:T(8,128)(2,1)}, bf16[30,120,128]{2,1,0:T(8,128)(2,1)}, u32[]{:S(2)}, u32[]{:S(2)}) %collective-permute-start.11) | collective-permute-done | bytes 921632 | tf_op jit(solution)/shard_map/ppermute | solution.py:468
  236.6 4.0 %fusion.3 = bf16[30,240,128]{2,1,0:T(8,128)(2,1)} fusion(f32[240,30,128,1]{2,0,3,1:T(8,128)S(1)} %fusion.54, bf16[30,240,128]{2,1,0:T(8,128)(2,1)} %get-tuple-element.42, bf16[30,120,128]{2,1,0:T(8,128)(2,1)} %collective-permute-done.11, f32[30]{0:T(128)S(1)} %get-tuple-element.119, bf16[240,120]{0,1:T(8,128)(2,1)S(1)} %reshape.615), kind=kOutput, calls=%fused_computation.14 | convolution fusion | flops 225792000 | bytes 8352120 | tf_op jit(solution)/shard_map/jkc,nk->jnc/dot_general | solution.py:633
  240.6 4.7 %collective-permute-start.17 = (bf16[30,240,128]{2,1,0:T(8,128)(2,1)}, bf16[30,240,128]{2,1,0:T(8,128)(2,1)}, u32[]{:S(2)}, u32[]{:S(2)}) collective-permute-start(bf16[30,240,128]{2,1,0:T(8,128)(2,1)} %fusion.3), channel_id=1, source_target_pairs={{8,0},{16,8},{24,16},{9,1},{17,9},{25,17},{10,2},{18,10},{26,18},{... | collective-permute-start | bytes 5529608 | tf_op jit(solution)/shard_map/ppermute | solution.py:22
  245.3 0.9 convert_add_fusion.1
  246.2 1.3 copy.123
  247.5 3.0 collective-permute-start.10
  250.8 0.9 fusion.95
  251.7 2.4 collective-permute-start.14
  254.1 0.9 fusion.52
  255.0 4.5 %collective-permute-done.14 = f32[2,120,128]{2,1,0:T(8,128)S(1)} collective-permute-done((f32[2,120,128]{2,1,0:T(8,128)S(1)}, f32[2,120,128]{2,1,0:T(8,128)S(1)}, u32[]{:S(2)}, u32[]{:S(2)}) %collective-permute-start.14) | collective-permute-done | bytes 122912 | tf_op jit(solution)/shard_map/ppermute | solution.py:468
  259.5 0.9 fusion.114
  260.5 19.1 %value_rows.3 = bf16[30,240,128]{2,1,0:T(8,128)(2,1)} custom-call(f32[60]{0:T(128)} %copy-done.18, bf16[60,240,128]{2,1,0:T(8,128)(2,1)} %bitcast.191, bf16[60,120,128]{2,1,0:T(8,128)(2,1)} %bitcast.201, bf16[30,120,128]{2,1,0:T(8,128)(2,1)} %collective-permute-done.12.far_ref, bf16[240,120]{1,0:T(8,128)(2,1)} %copy.98.inv_own_ref, ...), custom_call_target="tpu_custom_call" | custom-call | flops 5662310400 | bytes 7372800 | tf_op jit(solution)/shard_map/value_rows/pallas_call | solution.py:419
  279.6 4.1 %collective-permute-start.16 = (bf16[30,240,128]{2,1,0:T(8,128)(2,1)}, bf16[30,240,128]{2,1,0:T(8,128)(2,1)S(1)}, u32[]{:S(2)}, u32[]{:S(2)}) collective-permute-start(bf16[30,240,128]{2,1,0:T(8,128)(2,1)} %value_rows.3), channel_id=1, source_target_pairs={{0,8},{8,16},{16,24},{1,9},{9,17},{17,25},{2,10},{10,18},{18,26},{... | collective-permute-start | bytes 5529608 | tf_op jit(solution)/shard_map/ppermute | solution.py:22
  283.7 3.9 %fusion.1 = bf16[30,240,128]{2,1,0:T(8,128)(2,1)} fusion(f32[240,30,128,1]{2,0,3,1:T(8,128)S(1)} %fusion.52, bf16[30,240,128]{2,1,0:T(8,128)(2,1)} %get-tuple-element.60, bf16[30,120,128]{2,1,0:T(8,128)(2,1)} %collective-permute-done.18, f32[30]{0:T(128)S(1)} %get-tuple-element.118, bf16[240,120]{0,1:T(8,128)(2,1)S(1)} %copy-done.10), kind=kOutput, calls=%fused_computation.10 | convolution fusion | flops 225792000 | bytes 8352120 | tf_op jit(solution)/shard_map/jkc,nk->jnc/dot_general | solution.py:633
  287.6 1.9 collective-permute-start.19
  289.5 1.3 collective-permute-start.20
  292.3 1.0 collective-permute-done.20
  294.0 10.2 %collective-permute-done.16 = bf16[30,240,128]{2,1,0:T(8,128)(2,1)S(1)} collective-permute-done((bf16[30,240,128]{2,1,0:T(8,128)(2,1)}, bf16[30,240,128]{2,1,0:T(8,128)(2,1)S(1)}, u32[]{:S(2)}, u32[]{:S(2)}) %collective-permute-start.16) | collective-permute-done | bytes 1843232 | tf_op jit(solution)/shard_map/ppermute | solution.py:22
  304.3 3.7 %pad_maximum_fusion.6 = bf16[1,1,60,240,128]{4,3,2,1,0:T(8,128)(2,1)} fusion(bf16[1,1,30,240,128]{4,3,2,1,0:T(8,128)(2,1)S(1)} %bitcast.199, bf16[1,1,30,240,128]{4,3,2,1,0:T(8,128)(2,1)} %bitcast.51), kind=kLoop, calls=%fused_computation.6 | loop fusion | flops 1843200 | bytes 7372800 | tf_op jit(solution)/shard_map/dynamic_update_slice | solution.py:620
  307.9 4.6 %collective-permute-done.19 = bf16[30,240,128]{2,1,0:T(8,128)(2,1)} collective-permute-done((bf16[30,240,128]{2,1,0:T(8,128)(2,1)}, bf16[30,240,128]{2,1,0:T(8,128)(2,1)}, u32[]{:S(2)}, u32[]{:S(2)}) %collective-permute-start.19) | collective-permute-done | bytes 1843232 | tf_op jit(solution)/shard_map/ppermute | solution.py:22
  312.6 4.2 %pad_maximum_fusion.7 = bf16[1,1,60,240,128]{4,3,2,1,0:T(8,128)(2,1)} fusion(bf16[1,1,30,240,128]{4,3,2,1,0:T(8,128)(2,1)} %bitcast.68, bf16[1,1,30,240,128]{4,3,2,1,0:T(8,128)(2,1)} %bitcast.62), kind=kLoop, calls=%fused_computation.7 | loop fusion | flops 1843200 | bytes 7372800 | tf_op jit(solution)/shard_map/dynamic_update_slice | solution.py:620
  (123 shorter events, 18.7 us)
Async XLA Ops:
  5.3 42.3 %collective-permute-start.1 = (bf16[60,120,128]{2,1,0:T(8,128)(2,1)}, bf16[60,120,128]{2,1,0:T(8,128)(2,1)}, u32[]{:S(2)}, u32[]{:S(2)}) collective-permute-start(bf16[60,120,128]{2,1,0:T(8,128)(2,1)} %convert_bitcast_fusion.6), channel_id=1, source_target_pairs={{0,4},{4,0},{1,5},{5,1},{2,6},{6,2},{3,7},{7,3},{8,12},{12,8},{9,1... | collective-permute-start | bytes 5529608 | tf_op jit(solution)/shard_map/ppermute | solution.py:468
  7.9 186.4 %copy-start.11 = (bf16[240,1,60]{0,2,1:T(8,128)(2,1)}, bf16[240,1,60]{0,2,1:T(8,128)(2,1)S(1)}, u32[]{:S(2)}) copy-start(bf16[240,1,60]{0,2,1:T(8,128)(2,1)S(1)} %get-tuple-element.125) | copy-start | bytes 86404
  8.0 3.2 copy-start.1
  11.2 2.1 copy-start.19
  11.8 3.4 %copy-start.16 = (bf16[1,768,128]{2,1,0:T(8,128)(2,1)S(1)}, bf16[1,768,128]{2,1,0:T(8,128)(2,1)}, u32[]{:S(2)}) copy-start(bf16[1,768,128]{2,1,0:T(8,128)(2,1)} %param.11) | copy-start | bytes 589828
  11.9 4.2 %copy-start.15 = (bf16[1,128,768]{2,1,0:T(8,128)(2,1)S(1)}, bf16[1,128,768]{2,1,0:T(8,128)(2,1)}, u32[]{:S(2)}) copy-start(bf16[1,128,768]{2,1,0:T(8,128)(2,1)} %param.10) | copy-start | bytes 589828
  11.9 11.1 %copy-start.17 = (f32[1,2,120,128]{3,2,1,0:T(8,128)S(1)}, f32[1,2,120,128]{3,2,1,0:T(8,128)}, u32[]{:S(2)}) copy-start(f32[1,2,120,128]{3,2,1,0:T(8,128)} %param.12) | copy-start | bytes 368644
  13.2 141.2 %collective-permute-start = (bf16[30,120,128]{2,1,0:T(8,128)(2,1)}, bf16[30,120,128]{2,1,0:T(8,128)(2,1)}, u32[]{:S(2)}, u32[]{:S(2)}) collective-permute-start(bf16[30,120,128]{2,1,0:T(8,128)(2,1)} %get-tuple-element.35), channel_id=1, source_target_pairs={{0,4},{4,0},{1,5},{5,1},{2,6},{6,2},{3,7},{7,3},{8,12},{12,8},{9,1... | collective-permute-start | bytes 2764808 | tf_op jit(solution)/shard_map/ppermute | solution.py:468
  13.5 223.2 %copy-start.9 = (bf16[240,120]{0,1:T(8,128)(2,1)}, bf16[240,120]{0,1:T(8,128)(2,1)S(1)}, u32[]{:S(2)}) copy-start(bf16[240,120]{0,1:T(8,128)(2,1)S(1)} %reshape.615) | copy-start | bytes 172804
  13.6 35.7 %copy-start.13 = (bf16[240,120]{0,1:T(8,128)(2,1)}, bf16[240,120]{0,1:T(8,128)(2,1)S(1)}, u32[]{:S(2)}) copy-start(bf16[240,120]{0,1:T(8,128)(2,1)S(1)} %reshape.619) | copy-start | bytes 172804
  14.5 34.9 %copy-start.14 = (bf16[240,120]{0,1:T(8,128)(2,1)}, bf16[240,120]{0,1:T(8,128)(2,1)S(1)}, u32[]{:S(2)}) copy-start(bf16[240,120]{0,1:T(8,128)(2,1)S(1)} %reshape.618) | copy-start | bytes 172804
  17.0 32.4 %copy-start.18 = (f32[60]{0:T(128)}, f32[60]{0:T(128)S(1)}, u32[]{:S(2)}) copy-start(f32[60]{0:T(128)S(1)} %get-tuple-element.84.mask_ref) | copy-start | bytes 724
  50.5 3.1 copy-start
  55.3 2.6 copy-start.2
  56.6 30.3 %collective-permute-start.3 = (bf16[30,120,128]{2,1,0:T(8,128)(2,1)S(1)}, bf16[30,120,128]{2,1,0:T(8,128)(2,1)S(1)}, u32[]{:S(2)}, u32[]{:S(2)}) collective-permute-start(bf16[30,120,128]{2,1,0:T(8,128)(2,1)S(1)} %bitcast.211), channel_id=1, source_target_pairs={{0,4},{4,0},{1,5},{5,1},{2,6},{6,2},{3,7},{7,3},{8,12},{12,8},{9,1... | collective-permute-start | bytes 2764808 | tf_op jit(solution)/shard_map/ppermute | solution.py:468
  60.2 60.8 %collective-permute-start.4 = (bf16[30,120,128]{2,1,0:T(8,128)(2,1)}, bf16[30,120,128]{2,1,0:T(8,128)(2,1)}, u32[]{:S(2)}, u32[]{:S(2)}) collective-permute-start(bf16[30,120,128]{2,1,0:T(8,128)(2,1)} %bitcast.19), channel_id=1, source_target_pairs={{0,4},{4,0},{1,5},{5,1},{2,6},{6,2},{3,7},{7,3},{8,12},{12,8},{9,1... | collective-permute-start | bytes 2764808 | tf_op jit(solution)/shard_map/ppermute | solution.py:468
  65.2 89.2 %collective-permute-start.2 = (bf16[30,120,128]{2,1,0:T(8,128)(2,1)}, bf16[30,120,128]{2,1,0:T(8,128)(2,1)}, u32[]{:S(2)}, u32[]{:S(2)}) collective-permute-start(bf16[30,120,128]{2,1,0:T(8,128)(2,1)} %get-tuple-element.39), channel_id=1, source_target_pairs={{0,4},{4,0},{1,5},{5,1},{2,6},{6,2},{3,7},{7,3},{8,12},{12,8},{9,1... | collective-permute-start | bytes 2764808 | tf_op jit(solution)/shard_map/ppermute | solution.py:468
  86.9 0.9 copy-start.21
  119.8 55.4 %collective-permute-start.6 = (bf16[30,120,128]{2,1,0:T(8,128)(2,1)}, bf16[30,120,128]{2,1,0:T(8,128)(2,1)}, u32[]{:S(2)}, u32[]{:S(2)}) collective-permute-start(bf16[30,120,128]{2,1,0:T(8,128)(2,1)} %get-tuple-element.41), channel_id=1, source_target_pairs={{0,4},{4,0},{1,5},{5,1},{2,6},{6,2},{3,7},{7,3},{8,12},{12,8},{9,1... | collective-permute-start | bytes 2764808 | tf_op jit(solution)/shard_map/ppermute | solution.py:468
  154.1 21.1 %collective-permute-start.7 = (bf16[30,120,128]{2,1,0:T(8,128)(2,1)}, bf16[30,120,128]{2,1,0:T(8,128)(2,1)S(1)}, u32[]{:S(2)}, u32[]{:S(2)}) collective-permute-start(bf16[30,120,128]{2,1,0:T(8,128)(2,1)} %get-tuple-element.46), channel_id=1, source_target_pairs={{0,4},{4,0},{1,5},{5,1},{2,6},{6,2},{3,7},{7,3},{8,12},{12,8},{9,1... | collective-permute-start | bytes 2764808 | tf_op jit(solution)/shard_map/ppermute | solution.py:468
  154.5 10.9 %collective-permute-start.8 = (bf16[2,128,384]{2,1,0:T(8,128)(2,1)S(1)}, bf16[2,128,384]{2,1,0:T(8,128)(2,1)S(1)}, u32[]{:S(2)}, u32[]{:S(2)}) collective-permute-start(bf16[2,128,384]{2,1,0:T(8,128)(2,1)S(1)} %select_convert_fusion), channel_id=1, source_target_pairs={{0,2},{1,3},{2,0},{3,1},{4,6},{5,7},{6,4},{7,5},{8,10},{9,11},{10,... | collective-permute-start | bytes 589832 | tf_op jit(solution)/shard_map/ppermute | solution.py:468
  165.5 7.7 %collective-permute-start.9 = (bf16[2,128,192]{2,1,0:T(8,128)(2,1)S(1)}, bf16[2,128,192]{2,1,0:T(8,128)(2,1)S(1)}, u32[]{:S(2)}, u32[]{:S(2)}) collective-permute-start(bf16[2,128,192]{2,1,0:T(8,128)(2,1)S(1)} %select_convert_fusion.1), channel_id=1, source_target_pairs={{0,1},{1,0},{2,3},{3,2},{4,5},{5,4},{6,7},{7,6},{8,9},{9,8},{10,11... | collective-permute-start | bytes 294920 | tf_op jit(solution)/shard_map/ppermute | solution.py:468
  166.2 9.0 %copy-start.7 = (bf16[30,120,128]{2,1,0:T(8,128)(2,1)S(1)}, bf16[30,120,128]{2,1,0:T(8,128)(2,1)}, u32[]{:S(2)}) copy-start(bf16[30,120,128]{2,1,0:T(8,128)(2,1)} %get-tuple-element.43) | copy-start | bytes 2764804
  166.2 9.0 %copy-start.8 = (bf16[30,120,128]{2,1,0:T(8,128)(2,1)S(1)}, bf16[30,120,128]{2,1,0:T(8,128)(2,1)}, u32[]{:S(2)}) copy-start(bf16[30,120,128]{2,1,0:T(8,128)(2,1)} %get-tuple-element.49) | copy-start | bytes 2764804
  171.7 22.5 %collective-permute-start.5 = (bf16[30,120,128]{2,1,0:T(8,128)(2,1)S(1)}, bf16[30,120,128]{2,1,0:T(8,128)(2,1)S(1)}, u32[]{:S(2)}, u32[]{:S(2)}) collective-permute-start(bf16[30,120,128]{2,1,0:T(8,128)(2,1)S(1)} %bitcast.210), channel_id=1, source_target_pairs={{0,4},{4,0},{1,5},{5,1},{2,6},{6,2},{3,7},{7,3},{8,12},{12,8},{9,1... | collective-permute-start | bytes 2764808 | tf_op jit(solution)/shard_map/ppermute | solution.py:468
  172.9 87.5 %collective-permute-start.12 = (bf16[30,120,128]{2,1,0:T(8,128)(2,1)}, bf16[30,120,128]{2,1,0:T(8,128)(2,1)}, u32[]{:S(2)}, u32[]{:S(2)}) collective-permute-start(bf16[30,120,128]{2,1,0:T(8,128)(2,1)} %bitcast.42), channel_id=1, source_target_pairs={{0,4},{4,0},{1,5},{5,1},{2,6},{6,2},{3,7},{7,3},{8,12},{12,8},{9,1... | collective-permute-start | bytes 2764808 | tf_op jit(solution)/shard_map/ppermute | solution.py:468
  174.0 71.2 %collective-permute-start.15 = (bf16[2,128,192]{2,1,0:T(8,128)(2,1)}, bf16[2,128,192]{2,1,0:T(8,128)(2,1)}, u32[]{:S(2)}, u32[]{:S(2)}) collective-permute-start(bf16[2,128,192]{2,1,0:T(8,128)(2,1)} %get-tuple-element.80), channel_id=1, source_target_pairs={{0,4},{4,0},{1,5},{5,1},{2,6},{6,2},{3,7},{7,3},{8,12},{12,8},{9,1... | collective-permute-start | bytes 294920 | tf_op jit(solution)/shard_map/ppermute | solution.py:468
  175.2 3.6 %slice-start = ((s8[7372800]{0:T(1024)(128)(4,1)}), s8[4194304]{0:T(1024)(128)(4,1)S(1)}, s32[]{:S(2)}) async-start(s8[7372800]{0:T(1024)(128)(4,1)} %bitcast.186), calls=%async_computation | async-start | bytes 8388608
  177.7 1.9 slice-start.1
  181.8 1.4 copy-start.3
  181.8 1.4 copy-start.5
  182.5 68.3 %collective-permute-start.13 = (f32[2,120,128]{2,1,0:T(8,128)}, f32[2,120,128]{2,1,0:T(8,128)}, u32[]{:S(2)}, u32[]{:S(2)}) collective-permute-start(f32[2,120,128]{2,1,0:T(8,128)} %pad_maximum_fusion.14), channel_id=1, source_target_pairs={{0,1},{1,0},{2,3},{3,2},{4,5},{5,4},{6,7},{7,6},{8,9},{9,8},{10,11... | collective-permute-start | bytes 368648 | tf_op jit(solution)/shard_map/ppermute | solution.py:468
  186.8 49.8 %collective-permute-start.11 = (bf16[30,120,128]{2,1,0:T(8,128)(2,1)}, bf16[30,120,128]{2,1,0:T(8,128)(2,1)}, u32[]{:S(2)}, u32[]{:S(2)}) collective-permute-start(bf16[30,120,128]{2,1,0:T(8,128)(2,1)} %copy.118), channel_id=1, source_target_pairs={{0,4},{4,0},{1,5},{5,1},{2,6},{6,2},{3,7},{7,3},{8,12},{12,8},{9,1... | collective-permute-start | bytes 2764808 | tf_op jit(solution)/shard_map/ppermute | solution.py:468
  194.2 1.0 copy-start.20
  236.6 14.2 %copy-start.4 = (f32[120,128]{1,0:T(8,128)S(1)}, f32[120,128]{1,0:T(8,128)}, u32[]{:S(2)}) copy-start(f32[120,128]{1,0:T(8,128)} %copy-done.3) | copy-start | bytes 184324
  236.6 14.2 %copy-start.6 = (f32[120,128]{1,0:T(8,128)S(1)}, f32[120,128]{1,0:T(8,128)}, u32[]{:S(2)}) copy-start(f32[120,128]{1,0:T(8,128)} %copy-done.5) | copy-start | bytes 184324
  236.6 17.5 %copy-start.12 = (bf16[240,1,60]{0,2,1:T(8,128)(2,1)S(1)}, bf16[240,1,60]{0,2,1:T(8,128)(2,1)}, u32[]{:S(2)}) copy-start(bf16[240,1,60]{0,2,1:T(8,128)(2,1)} %copy-done.11) | copy-start | bytes 86404
  240.6 47.0 %collective-permute-start.17 = (bf16[30,240,128]{2,1,0:T(8,128)(2,1)}, bf16[30,240,128]{2,1,0:T(8,128)(2,1)}, u32[]{:S(2)}, u32[]{:S(2)}) collective-permute-start(bf16[30,240,128]{2,1,0:T(8,128)(2,1)} %fusion.3), channel_id=1, source_target_pairs={{8,0},{16,8},{24,16},{9,1},{17,9},{25,17},{10,2},{18,10},{26,18},{... | collective-permute-start | bytes 5529608 | tf_op jit(solution)/shard_map/ppermute | solution.py:22
  247.5 46.5 %collective-permute-start.10 = (bf16[30,240,128]{2,1,0:T(8,128)(2,1)}, bf16[30,240,128]{2,1,0:T(8,128)(2,1)}, u32[]{:S(2)}, u32[]{:S(2)}) collective-permute-start(bf16[30,240,128]{2,1,0:T(8,128)(2,1)} %value_rows.2), channel_id=1, source_target_pairs={{0,8},{8,16},{16,24},{1,9},{9,17},{17,25},{2,10},{10,18},{18,26},{... | collective-permute-start | bytes 5529608 | tf_op jit(solution)/shard_map/ppermute | solution.py:22
  250.5 33.2 %collective-permute-start.18 = (bf16[30,120,128]{2,1,0:T(8,128)(2,1)}, bf16[30,120,128]{2,1,0:T(8,128)(2,1)}, u32[]{:S(2)}, u32[]{:S(2)}) collective-permute-start(bf16[30,120,128]{2,1,0:T(8,128)(2,1)} %copy.123), channel_id=1, source_target_pairs={{0,4},{4,0},{1,5},{5,1},{2,6},{6,2},{3,7},{7,3},{8,12},{12,8},{9,1... | collective-permute-start | bytes 2764808 | tf_op jit(solution)/shard_map/ppermute | solution.py:468
  251.7 7.8 %collective-permute-start.14 = (f32[2,120,128]{2,1,0:T(8,128)S(1)}, f32[2,120,128]{2,1,0:T(8,128)S(1)}, u32[]{:S(2)}, u32[]{:S(2)}) collective-permute-start(f32[2,120,128]{2,1,0:T(8,128)S(1)} %fusion.95), channel_id=1, source_target_pairs={{0,2},{1,3},{2,0},{3,1},{4,6},{5,7},{6,4},{7,5},{8,10},{9,11},{10,... | collective-permute-start | bytes 368648 | tf_op jit(solution)/shard_map/ppermute | solution.py:468
  260.5 23.3 %copy-start.10 = (bf16[240,120]{0,1:T(8,128)(2,1)S(1)}, bf16[240,120]{0,1:T(8,128)(2,1)}, u32[]{:S(2)}) copy-start(bf16[240,120]{0,1:T(8,128)(2,1)} %copy-done.9) | copy-start | bytes 172804
  279.6 24.6 %collective-permute-start.16 = (bf16[30,240,128]{2,1,0:T(8,128)(2,1)}, bf16[30,240,128]{2,1,0:T(8,128)(2,1)S(1)}, u32[]{:S(2)}, u32[]{:S(2)}) collective-permute-start(bf16[30,240,128]{2,1,0:T(8,128)(2,1)} %value_rows.3), channel_id=1, source_target_pairs={{0,8},{8,16},{16,24},{1,9},{9,17},{17,25},{2,10},{10,18},{18,26},{... | collective-permute-start | bytes 5529608 | tf_op jit(solution)/shard_map/ppermute | solution.py:22
  287.6 24.9 %collective-permute-start.19 = (bf16[30,240,128]{2,1,0:T(8,128)(2,1)}, bf16[30,240,128]{2,1,0:T(8,128)(2,1)}, u32[]{:S(2)}, u32[]{:S(2)}) collective-permute-start(bf16[30,240,128]{2,1,0:T(8,128)(2,1)} %fusion.1), channel_id=1, source_target_pairs={{8,0},{16,8},{24,16},{9,1},{17,9},{25,17},{10,2},{18,10},{26,18},{... | collective-permute-start | bytes 5529608 | tf_op jit(solution)/shard_map/ppermute | solution.py:22
  289.5 3.8 %collective-permute-start.20 = (f32[2,120,128]{2,1,0:T(8,128)S(1)}, f32[2,120,128]{2,1,0:T(8,128)S(1)}, u32[]{:S(2)}, u32[]{:S(2)}) collective-permute-start(f32[2,120,128]{2,1,0:T(8,128)S(1)} %fusion.114), channel_id=1, source_target_pairs={{0,4},{4,0},{1,5},{5,1},{2,6},{6,2},{3,7},{7,3},{8,12},{12,8},{9,1... | collective-permute-start | bytes 368648 | tf_op jit(solution)/shard_map/ppermute | solution.py:468
